TPU v7x, 256 devices: a whole 4x4x8 slice. The times are simulated.
256 devices in a mesh: dp: 4 (over x), rows: 64 (over y, z, core).
Axes of the slice: x: 4, y: 4, z: 8, core: 2. Of those that a mesh axis runs over, the one named last changes fastest.
Arguments:
- grads: bfloat16 [4, 64, 1024, 1024], P('dp', None, 'rows'), may hold values from -6 to 6
- weight: bfloat16 [64, 1024, 1024], P(None, 'rows'), may hold values from -6 to 6
- basis: float32 [64, 1024, 256], P(None, 'rows'), may hold values from -6 to 6
- first_moment: float32 [256, 256, 1024], P('rows', None, 'dp'), may hold values from -6 to 6
- second_moment: float32 [256, 256, 1024], P('rows', None, 'dp'), may hold values from 0.5 to 4
- sketch: bfloat16 [1024, 256], replicated, may hold values from -6 to 6
- owner: int32 [64], replicated, may hold values from 0 to 63, as said below
- rank: int32 [64], replicated, may hold values from 128 to 256
Outputs:
- new_weight: bfloat16 [64, 1024, 1024], P(None, 'rows')
- new_basis: float32 [64, 1024, 256], P(None, 'rows')
- first_out: float32 [256, 256, 1024], P('rows', None, 'dp')
- second_out: float32 [256, 256, 1024], P('rows', None, 'dp')
Inputs may be any that keep to these rules, and one draw needn't show every extreme that they name: No owner is named by more than 4 matrices, and some owner is named by exactly 4.
All inputs are finite; a program needn't handle non-finite values.
Results may differ from a plain program's by a relative error of at most 0.012.
Values may be sent and summed in bfloat16 or wider, within the bound.
A program may use at most 128 MiB of HBM per device.

v0:
```python
import jax
import jax.numpy as jnp
from jax import lax
from jax.sharding import PartitionSpec as P

beta_one = 0.9
beta_two = 0.95
bias_one = 1.0 - 0.9**10
bias_two = 1.0 - 0.95**10
step_size = 0.5
epsilon = 1e-08


def slot_of(owner, capacity):
    same = owner[:, None] == owner[None, :]
    places = jnp.arange(owner.shape[0], dtype=jnp.int32)
    earlier = places[None, :] < places[:, None]
    within = jnp.sum((same & earlier).astype(jnp.int32), axis=1)
    return owner * capacity + within


def spread_half(placing, data, capacity, owners):
    flat = data.reshape(data.shape[0], -1)
    moved = jnp.dot(placing.T, flat, preferred_element_type=jnp.float32).astype(jnp.bfloat16)
    return moved.reshape(capacity, owners, data.shape[1], data.shape[2])


def spread_full(placing, data, capacity, owners):
    flat = data.reshape(data.shape[0], -1)
    moved = jnp.dot(placing.T, flat, precision=lax.Precision.HIGHEST)
    return moved.reshape(capacity, owners, data.shape[1], data.shape[2])


def collect_half(placing, data):
    flat = data.reshape(placing.shape[1], -1)
    picked = jnp.dot(placing, flat, preferred_element_type=jnp.float32).astype(jnp.bfloat16)
    return picked.reshape(placing.shape[0], data.shape[2], data.shape[3])


def collect_full(placing, data):
    flat = data.reshape(placing.shape[1], -1)
    picked = jnp.dot(placing, flat, precision=lax.Precision.HIGHEST)
    return picked.reshape(placing.shape[0], data.shape[2], data.shape[3])


def per_device(grads, weight, basis, first_moment, second_moment, sketch, owner, rank):
    owners = lax.axis_size("rows")
    here = lax.axis_index("rows")
    group = lax.axis_index("dp")
    capacity = first_moment.shape[0]
    rank_full = first_moment.shape[1]
    quarter = first_moment.shape[2]
    shard = weight.shape[1]
    width = weight.shape[2]
    total_rows = shard * owners
    root = float(total_rows) ** 0.5
    inverse_root = float(total_rows) ** (-0.5)
    slots = slot_of(owner, capacity)
    column = slots % capacity * owners + slots // capacity
    placing = column[:, None] == jnp.arange(capacity * owners, dtype=jnp.int32)[None, :]
    place_half = placing.astype(jnp.bfloat16)
    place_full = placing.astype(jnp.float32)
    sent_basis = lax.all_to_all(
        spread_full(place_full, basis, capacity, owners),
        "rows",
        split_axis=1,
        concat_axis=1,
        tiled=True,
    )
    old_basis = sent_basis.reshape(capacity, total_rows, rank_full)
    total = lax.psum(grads[0], "dp").astype(jnp.float32).astype(jnp.bfloat16)
    sent_grad = lax.all_to_all(
        spread_half(place_half, total, capacity, owners),
        "rows",
        split_axis=1,
        concat_axis=1,
        tiled=True,
    )
    whole = sent_grad.reshape(capacity, total_rows, width)
    own = lax.dynamic_slice_in_dim(whole, group * quarter, quarter, 2)
    sample = jnp.einsum("cmd,dr->cmr", whole, sketch, preferred_element_type=jnp.float32)
    matched = slots[:, None] == (here * capacity + jnp.arange(capacity, dtype=jnp.int32))[None, :]
    valid = jnp.any(matched, axis=0).astype(jnp.float32)
    rank_slot = jnp.sum(jnp.where(matched, rank[:, None], 0), axis=0)
    projected = (
        jnp.einsum(
            "cmr,cmd->crd", old_basis, own.astype(jnp.float32), precision=lax.Precision.HIGHEST
        )
        * inverse_root
    )
    first_new = beta_one * first_moment + (1.0 - beta_one) * projected
    second_new = beta_two * second_moment + (1.0 - beta_two) * projected * projected
    keeping = (jnp.arange(rank_full, dtype=jnp.int32)[None, :] < rank_slot[:, None]).astype(
        jnp.float32
    )[:, :, None]
    update = keeping * (first_new / bias_one) / (jnp.sqrt(second_new / bias_two) + epsilon)
    delta = (
        jnp.einsum("cmr,crd->cmd", old_basis, update, precision=lax.Precision.HIGHEST)
        * inverse_root
    ).astype(jnp.bfloat16)
    gram = jnp.einsum("cmr,cms->crs", sample, sample, precision=lax.Precision.HIGHEST)
    gram = gram + (1.0 - valid)[:, None, None] * jnp.eye(rank_full, dtype=jnp.float32)[None, :, :]
    lower = jnp.linalg.cholesky(gram)
    new_basis = (
        lax.linalg.triangular_solve(lower, sample, left_side=False, lower=True, transpose_a=True)
        * root
    )
    back_delta = lax.all_to_all(
        delta.reshape(capacity, owners, shard, quarter),
        "rows",
        split_axis=1,
        concat_axis=1,
        tiled=True,
    )
    full_delta = lax.all_gather(collect_half(place_half, back_delta), "dp", axis=2, tiled=True)
    back_basis = lax.all_to_all(
        new_basis.reshape(capacity, owners, shard, rank_full),
        "rows",
        split_axis=1,
        concat_axis=1,
        tiled=True,
    )
    mine_basis = collect_full(place_full, back_basis)
    new_weight = (weight.astype(jnp.float32) - step_size * full_delta.astype(jnp.float32)).astype(
        jnp.bfloat16
    )
    scale_slot = valid[:, None, None]
    return (new_weight, mine_basis, first_new * scale_slot, second_new * scale_slot)


def solution(mesh):
    in_specs = (
        P("dp", None, "rows", None),
        P(None, "rows", None),
        P(None, "rows", None),
        P("rows", None, "dp"),
        P("rows", None, "dp"),
        P(),
        P(),
        P(),
    )
    out_specs = (
        P(None, "rows", None),
        P(None, "rows", None),
        P("rows", None, "dp"),
        P("rows", None, "dp"),
    )
    return jax.shard_map(
        per_device, mesh=mesh, in_specs=in_specs, out_specs=out_specs, check_vma=False
    )
```

profile of v0, /device:TPU:1, one launch (start us, length us, event | category | flops | bytes accessed | tf_op | source)
XLA Modules:
  0.0 740.5 jit_solution(191552147987780826)
XLA Ops:
  7.2 0.9 convert_reduce_fusion
  8.1 0.7 fusion.41
  8.8 3.5 fusion.5
  12.3 4.4 copy.72
  16.7 13.5 %all-to-all-start = ((f32[4,64,16,256]{3,2,0,1:T(8,128)}), f32[4,64,16,256]{3,2,0,1:T(8,128)}, u32[]{:S(2)}, u32[]{:S(2)}) async-start(f32[4,64,16,256]{3,2,0,1:T(8,128)} %copy.72), calls=%async_computation | async-start | bytes 8388608 | tf_op jit(solution)/shard_map/all_to_all | solution.py:63
  30.4 2.6 copy.105
  33.1 65.7 %all-reduce.3.cloned.1.call-done = bf16[64,16384]{1,0:T(8,128)(2,1)} async-done(((bf16[64,16384]{1,0:T(8,128)(2,1)}), bf16[64,16384]{1,0:T(8,128)(2,1)}) %all-reduce.3.cloned.1.call-update) | async-done | bytes 2097168 | tf_op jit(solution)/shard_map/psum | solution.py:71
  98.7 7.3 convolution_convert_fusion
  106.0 15.6 %copy.106 = bf16[32,8,16,1024]{3,2,1,0:T(8,128)(2,1)} copy(bf16[32,8,16,1024]{3,1,2,0:T(8,128)(2,1)} %bitcast.92) | data formatting | bytes 16777216
  121.6 8.5 %copy.74 = bf16[4,64,16,1024]{3,2,0,1:T(8,128)(2,1)} copy(bf16[4,64,16,1024]{3,2,1,0:T(8,128)(2,1)} %bitcast.93) | data formatting | bytes 16777216 | tf_op jit(solution)/shard_map/reshape | solution.py:25
  130.2 11.0 %all-to-all-start.1 = ((bf16[4,64,16,1024]{3,2,0,1:T(8,128)(2,1)}), bf16[4,64,16,1024]{3,2,0,1:T(8,128)(2,1)}, u32[]{:S(2)}, u32[]{:S(2)}) async-start(bf16[4,64,16,1024]{3,2,0,1:T(8,128)(2,1)} %copy.74), calls=%async_computation.1 | async-start | bytes 16777216 | tf_op jit(solution)/shard_map/all_to_all | solution.py:72
  141.8 4.8 copy.73
  146.6 180.4 %all-to-all-done.1 = bf16[4,64,16,1024]{3,2,0,1:T(8,128)(2,1)} async-done(((bf16[4,64,16,1024]{3,2,0,1:T(8,128)(2,1)}), bf16[4,64,16,1024]{3,2,0,1:T(8,128)(2,1)}, u32[]{:S(2)}, u32[]{:S(2)}) %all-to-all-start.1) | async-done | bytes 8388640 | tf_op jit(solution)/shard_map/all_to_all | solution.py:72
  327.0 8.5 %copy.75 = bf16[4,64,16,1024]{3,2,1,0:T(8,128)(2,1)} copy(bf16[4,64,16,1024]{3,2,0,1:T(8,128)(2,1)} %all-to-all-done.1) | data formatting | bytes 16777216 | tf_op jit(solution)/shard_map/all_to_all | solution.py:72
  335.5 7.8 %fusion.14 = f32[4,1024,256]{2,1,0:T(8,128)} fusion(bf16[4,1024,1024]{2,1,0:T(8,128)(2,1)} %bitcast.100, bf16[1024,256]{1,0:T(8,128)(2,1)S(1)} %copy-done), kind=kOutput, calls=%fused_computation.29 | convolution fusion | flops 2147483648 | bytes 13107200 | tf_op jit(solution)/shard_map/cmd,dr->cmr/dot_general | solution.py:81
  343.4 6.8 broadcast_multiply_fusion
  350.2 4.7 multiply_convert_fusion
  354.9 1.6 copy.77
  356.6 6.4 all-to-all-start.2
  363.0 10.0 %fusion.50 = f32[4,256,256]{2,1,0:T(8,128)S(1)} fusion(f32[4,1024,256]{2,1,0:T(8,128)} %fusion.14), kind=kOutput, calls=%fused_computation.97 | convolution fusion | flops 3221225472 | bytes 5242880 | tf_op jit(solution)/shard_map/cmr,cms->crs/dot_general | solution.py:101
  373.6 1.0 copy-done.4
  374.6 46.9 %custom-call.16 = f32[4,128,128]{2,1,0:T(8,128)S(1)} custom-call(f32[4,128,128]{2,1,0:T(8,128)S(1)} %cholesky.122), custom_call_target="Cholesky" | custom-call | tf_op jit(solution)/shard_map/jit(cholesky)/cholesky | solution.py:103
  421.7 39.3 %custom-call.17 = f32[4,1,128,128]{2,3,1,0:T(8,128)S(1)} custom-call(f32[4,1,128,128]{3,2,1,0:T(8,128)S(1)} %select_bitcast_fusion), custom_call_target="InvertDiagBlocksLowerTriangular" | custom-call | tf_op jit(solution)/shard_map/jit(cholesky)/cholesky | solution.py:103
  461.0 1.4 constant_dynamic-update-slice_fusion.1
  462.3 1.6 convolution_subtract_fusion
  464.0 47.1 %custom-call.18 = f32[4,128,128]{2,1,0:T(8,128)S(1)} custom-call(f32[4,128,128]{2,1,0:T(8,128)S(1)} %convolution_subtract_fusion), custom_call_target="Cholesky" | custom-call | tf_op jit(solution)/shard_map/jit(cholesky)/cholesky | solution.py:103
  511.7 5.3 while.1
  511.7 0.6 fusion.63
  512.3 2.1 bitcast_dynamic-update-slice_fusion.2
  514.3 0.6 fusion.63
  514.9 2.1 bitcast_dynamic-update-slice_fusion.2
  517.0 79.4 %custom-call.19 = f32[4,2,128,128]{2,3,1,0:T(8,128)S(1)} custom-call(f32[4,2,128,128]{3,2,1,0:T(8,128)} %bitcast.111), custom_call_target="InvertDiagBlocksLowerTriangular" | custom-call | tf_op jit(solution)/shard_map/triangular_solve | solution.py:105
  596.4 3.7 fusion.1
  600.1 1.9 fusion.19
  602.1 2.0 fusion
  604.1 2.5 copy_multiply_fusion
  606.5 10.5 %all-to-all-start.3 = ((f32[4,64,16,256]{3,2,0,1:T(8,128)}), f32[4,64,16,256]{3,2,0,1:T(8,128)}, u32[]{:S(2)}, u32[]{:S(2)}) async-start(f32[4,64,16,256]{3,2,0,1:T(8,128)} %copy_multiply_fusion), calls=%async_computation.3 | async-start | bytes 8388608 | tf_op jit(solution)/shard_map/all_to_all | solution.py:116
  617.4 1.8 copy.78
  619.2 0.9 copy.107
  620.6 0.9 copy.108
  621.6 35.8 %all-gather.2.cloned.1.call-done = bf16[64,16,1024]{2,1,0:T(8,128)(2,1)} async-done(((bf16[64,16,256]{2,1,0:T(8,128)(2,1)}), bf16[64,16,1024]{2,1,0:T(8,128)(2,1)}) %all-gather.2.cloned.1.call-update) | async-done | bytes 2097168 | tf_op jit(solution)/shard_map/all_gather | solution.py:115
  657.3 3.9 subtract_convert_fusion
  661.2 51.7 %all-to-all-done.3 = f32[4,64,16,256]{3,2,0,1:T(8,128)} async-done(((f32[4,64,16,256]{3,2,0,1:T(8,128)}), f32[4,64,16,256]{3,2,0,1:T(8,128)}, u32[]{:S(2)}, u32[]{:S(2)}) %all-to-all-start.3) | async-done | bytes 4194336 | tf_op jit(solution)/shard_map/all_to_all | solution.py:116
  712.9 2.8 copy.88
  715.7 5.7 copy.109
  721.5 5.7 copy.89
  727.1 4.5 fusion.31
  731.6 1.6 copy.90
  (52 shorter events, 3.0 us)
Async XLA Ops:
  7.2 328.4 %copy-start = (bf16[1024,256]{1,0:T(8,128)(2,1)S(1)}, bf16[1024,256]{1,0:T(8,128)(2,1)}, u32[]{:S(2)}) copy-start(bf16[1024,256]{1,0:T(8,128)(2,1)} %param.13) | copy-start | bytes 1572868
  16.7 13.8 %copy-start.6 = (bf16[1,64,16,1024]{3,2,1,0:T(8,128)(2,1)S(1)}, bf16[1,64,16,1024]{3,2,1,0:T(8,128)(2,1)}, u32[]{:S(2)}) copy-start(bf16[1,64,16,1024]{3,2,1,0:T(8,128)(2,1)} %param.8) | copy-start | bytes 6291460
  16.7 113.5 %all-to-all-start = ((f32[4,64,16,256]{3,2,0,1:T(8,128)}), f32[4,64,16,256]{3,2,0,1:T(8,128)}, u32[]{:S(2)}, u32[]{:S(2)}) async-start(f32[4,64,16,256]{3,2,0,1:T(8,128)} %copy.72), calls=%async_computation | async-start | bytes 8388608 | tf_op jit(solution)/shard_map/all_to_all | solution.py:63
  30.2 68.6 %all-reduce.3.cloned.1.call-start = ((), (), s32[]{:S(2)}) async-start(), calls=%async_computation.4 | async-start | bytes 4194304 | tf_op jit(solution)/shard_map/psum | solution.py:71
  130.2 11.3 %copy-start.9 = (s32[64]{0:T(128)S(1)}, s32[64]{0:T(128)}, u32[]{:S(2)}) copy-start(s32[64]{0:T(128)} %param.15) | copy-start | bytes 772
  130.2 196.8 %all-to-all-start.1 = ((bf16[4,64,16,1024]{3,2,0,1:T(8,128)(2,1)}), bf16[4,64,16,1024]{3,2,0,1:T(8,128)(2,1)}, u32[]{:S(2)}, u32[]{:S(2)}) async-start(bf16[4,64,16,1024]{3,2,0,1:T(8,128)(2,1)} %copy.74), calls=%async_computation.1 | async-start | bytes 16777216 | tf_op jit(solution)/shard_map/all_to_all | solution.py:72
  335.5 7.9 %copy-start.3 = (f32[4,64,16,256]{3,2,1,0:T(8,128)S(1)}, f32[4,64,16,256]{3,2,1,0:T(8,128)}, u32[]{:S(2)}) copy-start(f32[4,64,16,256]{3,2,1,0:T(8,128)} %copy.73) | copy-start | bytes 12582916
  335.5 7.9 %copy-start.7 = (f32[4,256,256]{2,1,0:T(8,128)S(1)}, f32[4,256,256]{2,1,0:T(8,128)}, u32[]{:S(2)}) copy-start(f32[4,256,256]{2,1,0:T(8,128)} %param.12) | copy-start | bytes 3145732
  335.5 7.9 %copy-start.8 = (f32[4,256,256]{2,1,0:T(8,128)S(1)}, f32[4,256,256]{2,1,0:T(8,128)}, u32[]{:S(2)}) copy-start(f32[4,256,256]{2,1,0:T(8,128)} %param.11) | copy-start | bytes 3145732
  356.6 250.0 %all-to-all-start.2 = ((bf16[4,64,16,256]{3,2,0,1:T(8,128)(2,1)}), bf16[4,64,16,256]{3,2,0,1:T(8,128)(2,1)}, u32[]{:S(2)}, u32[]{:S(2)}) async-start(bf16[4,64,16,256]{3,2,0,1:T(8,128)(2,1)} %copy.77), calls=%async_computation.2 | async-start | bytes 4194304 | tf_op jit(solution)/shard_map/all_to_all | solution.py:108
  373.6 1.0 copy-start.4
  596.4 5.6 copy-start.2
  606.5 106.4 %all-to-all-start.3 = ((f32[4,64,16,256]{3,2,0,1:T(8,128)}), f32[4,64,16,256]{3,2,0,1:T(8,128)}, u32[]{:S(2)}, u32[]{:S(2)}) async-start(f32[4,64,16,256]{3,2,0,1:T(8,128)} %copy_multiply_fusion), calls=%async_computation.3 | async-start | bytes 8388608 | tf_op jit(solution)/shard_map/all_to_all | solution.py:116
  617.1 40.3 %all-gather.2.cloned.1.call-start = ((), (), s32[]{:S(2)}) async-start(), calls=%async_computation.5 | async-start | bytes 2621440 | tf_op jit(solution)/shard_map/all_gather | solution.py:115
  619.1 38.2 %copy-start.5 = (bf16[64,16,1024]{2,1,0:T(8,128)(2,1)S(1)}, bf16[64,16,1024]{2,1,0:T(8,128)(2,1)}, u32[]{:S(2)}) copy-start(bf16[64,16,1024]{2,1,0:T(8,128)(2,1)} %param.9) | copy-start | bytes 6291460
  721.5 11.7 %copy-start.1 = (bf16[1024,256]{1,0:T(8,128)(2,1)S(1)}, bf16[1024,256]{1,0:T(8,128)(2,1)}, u32[]{:S(2)}) copy-start(bf16[1024,256]{1,0:T(8,128)(2,1)} %param.13) | copy-start | bytes 1572868
Sparse Core Ops, SparseCore 0:
  33.9 64.7 all-reduce.2
  621.7 35.6 all-gather.1
where the time goes:
time: 746 us; the launch traced here: 740 us
  waiting for transfers between devices  334 us (45%)
  other arithmetic  222 us (30%)
  local copies, waits for them, and re-layouts  72.4 us (10%)
  matrix products  55.7 us (7%)
  starting transfers between devices  42 us (6%)
  between operations  14.8 us (2%)
    all_to_all x1, waiting for transfers between devices, per_device(): lax.all_to_all(spread_half(place_half, total, capacity, owners), 'rows',...  180 us
    another operation x10, other arithmetic, per_device(): lower = jnp.linalg.cholesky(gram)  134 us
    another operation x4, other arithmetic, per_device(): lax.linalg.triangular_solve(lower, sample, left_side=False, lower=True, t...  79.6 us
    psum x1, waiting for transfers between devices, per_device(): total = lax.psum(grads[0], 'dp').astype(jnp.float32).astype(jnp.bfloat16)  65.7 us
    all_to_all x1, waiting for transfers between devices, per_device(): lax.all_to_all(new_basis.reshape(capacity, owners, shard, rank_full), 'ro...  51.7 us
    all_gather x1, waiting for transfers between devices, per_device(): lax.all_gather(collect_half(place_half, back_delta), 'dp', axis=2, tiled=...  35.8 us
    unnamed x26, local copies, waits for them, and re-layouts  28.4 us
  transfers between devices with their start and end apart: 6, of which 4 were waited for; matrix products, arithmetic and copies ran while one was open for 39% of the time, Pallas kernels for 0%

commit v1 on v0

v1 whole, which is shorter than its diff:
```python
import jax
import jax.numpy as jnp
from jax import lax
from jax.experimental import pallas as pl
from jax.experimental.pallas import tpu as pltpu
from jax.sharding import PartitionSpec as P

beta_one = 0.9
beta_two = 0.95
bias_one = 1.0 - 0.9**10
bias_two = 1.0 - 0.95**10
step_size = 0.5
epsilon = 1e-08

PANEL = 32


def slot_of(owner, capacity):
    same = owner[:, None] == owner[None, :]
    places = jnp.arange(owner.shape[0], dtype=jnp.int32)
    earlier = places[None, :] < places[:, None]
    within = jnp.sum((same & earlier).astype(jnp.int32), axis=1)
    return owner * capacity + within


def inverse_factor_kernel(gram_ref, out_ref, work_ref):
    size = gram_ref.shape[0]
    wide = 2 * size
    work_ref[:, :size] = gram_ref[...]
    row = lax.broadcasted_iota(jnp.int32, (size, size), 0)
    col = lax.broadcasted_iota(jnp.int32, (size, size), 1)
    work_ref[:, size:] = jnp.where(row == col, 1.0, 0.0)
    lane = lax.broadcasted_iota(jnp.int32, (PANEL, 128), 1)
    below = lax.broadcasted_iota(jnp.int32, (PANEL, 128), 0)
    unit = jnp.where(lane == below + PANEL, 1.0, 0.0)
    wide_lane = lax.broadcasted_iota(jnp.int32, (PANEL, size), 1)

    def panel(step, carry):
        head = work_ref[:PANEL, :]
        aug = jnp.where(lane < PANEL, head[:, :128], unit)
        scale = jnp.zeros((PANEL, 128), jnp.float32)
        for j in range(PANEL):
            pivot_row = aug[j : j + 1, :]
            column = jnp.broadcast_to(aug[:, j : j + 1], (PANEL, 128))
            pivot = column[j : j + 1, :]
            factor = jnp.where(below > j, column / pivot, 0.0)
            scale = jnp.where(below == j, lax.rsqrt(pivot), scale)
            aug = aug - factor * pivot_row
        inverse = (aug * scale)[:, PANEL : 2 * PANEL]
        solved = jnp.dot(
            inverse, head, precision=lax.Precision.HIGHEST, preferred_element_type=jnp.float32
        )
        rolled = pltpu.roll(solved, lax.rem(step * PANEL + size, wide), axis=1)
        out_ref[pl.ds(pl.multiple_of(step * PANEL, PANEL), PANEL), :] = rolled[:, :size]
        left = jnp.where(wide_lane < size - step * PANEL, solved[:, :size], 0.0)
        change = lax.dot_general(
            left,
            solved,
            (((0,), (0,)), ((), ())),
            precision=lax.Precision.HIGHEST,
            preferred_element_type=jnp.float32,
        )
        fresh = work_ref[PANEL:, :] - change[PANEL:, :]
        work_ref[: size - PANEL, :] = pltpu.roll(fresh, wide - PANEL, axis=1)
        return carry

    lax.fori_loop(0, size // PANEL, panel, 0)


def inverse_factor(gram):
    size = gram.shape[0]
    return pl.pallas_call(
        inverse_factor_kernel,
        out_shape=jax.ShapeDtypeStruct((size, size), jnp.float32),
        in_specs=[pl.BlockSpec(memory_space=pltpu.VMEM)],
        out_specs=pl.BlockSpec(memory_space=pltpu.VMEM),
        scratch_shapes=[pltpu.VMEM((size, 2 * size), jnp.float32)],
        cost_estimate=pl.CostEstimate(
            flops=20000000000, bytes_accessed=8 * size * size, transcendentals=0
        ),
        name="inverse_factor",
    )(gram)


def pick_kernel(index_ref, data_ref, out_ref):
    count = out_ref.shape[0]

    def one(i, carry):
        place = index_ref[i]
        block = data_ref[jnp.maximum(place, 0)]
        out_ref[i] = jnp.where(place >= 0, block, jnp.zeros_like(block))
        return carry

    lax.fori_loop(0, count, one, 0, unroll=4)


def pick(index, data):
    return pl.pallas_call(
        pick_kernel,
        out_shape=jax.ShapeDtypeStruct((index.shape[0],) + data.shape[1:], data.dtype),
        in_specs=[
            pl.BlockSpec(memory_space=pltpu.SMEM),
            pl.BlockSpec(memory_space=pltpu.VMEM),
        ],
        out_specs=pl.BlockSpec(memory_space=pltpu.VMEM),
        name="pick",
    )(index, data)


def to_chunks(data):
    rows, cols = data.shape[-2:]
    lead = data.shape[:-2]
    n = len(lead)
    tiles = data.reshape(lead + (rows // 8, 8, cols // 128, 128))
    tiles = jnp.transpose(tiles, tuple(range(n)) + (n, n + 2, n + 1, n + 3))
    return tiles.reshape(lead + (rows // 8 * (cols // 128), 8, 128))


def from_chunks(data, rows, cols):
    lead = data.shape[:-3]
    n = len(lead)
    tiles = data.reshape(lead + (rows // 8, cols // 128, 8, 128))
    tiles = jnp.transpose(tiles, tuple(range(n)) + (n, n + 2, n + 1, n + 3))
    return tiles.reshape(lead + (rows, cols))


def exchange(data, axis=0):
    return lax.all_to_all(data, "rows", split_axis=axis, concat_axis=axis, tiled=True)


def per_device(grads, weight, basis, first_moment, second_moment, sketch, owner, rank):
    owners = lax.axis_size("rows")
    groups = lax.axis_size("dp")
    here = lax.axis_index("rows")
    capacity, rank_full, quarter = first_moment.shape
    count, shard, width = weight.shape
    total_rows = shard * owners
    root = float(total_rows) ** 0.5
    inverse_root = float(total_rows) ** (-0.5)
    slots = slot_of(owner, capacity)
    column = slots % capacity * owners + slots // capacity
    column_ids = jnp.arange(capacity * owners, dtype=jnp.int32)
    hit = column[:, None] == column_ids[None, :]
    matrix_ids = jnp.arange(count, dtype=jnp.int32)
    source = jnp.max(jnp.where(hit, matrix_ids[:, None], -1), axis=0)

    parts = jnp.transpose(grads[0].reshape(count, shard, groups, quarter), (2, 0, 1, 3))
    parts = lax.all_to_all(parts, "dp", split_axis=0, concat_axis=0, tiled=True)
    mine = jnp.sum(parts.astype(jnp.float32), axis=0).astype(jnp.bfloat16)

    old_basis = exchange(basis.astype(jnp.bfloat16)).reshape(total_rows, rank_full)

    moments = jnp.stack(
        [
            to_chunks(first_moment.astype(jnp.bfloat16)),
            to_chunks(second_moment.astype(jnp.bfloat16)),
        ],
        axis=2,
    )
    moments = exchange(moments, axis=1)
    moments = pick(column, moments.reshape(capacity * owners, 16, 128))
    moments = exchange(moments).reshape(owners, 2, 8, 128)
    first_old = from_chunks(moments[:, 0], rank_full, quarter).astype(jnp.float32)
    second_old = from_chunks(moments[:, 1], rank_full, quarter).astype(jnp.float32)

    own = exchange(mine).reshape(total_rows, quarter)
    whole = lax.all_gather(own, "dp", axis=1, tiled=True)

    projected = (
        lax.dot_general(
            old_basis, own, (((0,), (0,)), ((), ())), preferred_element_type=jnp.float32
        )
        * inverse_root
    )
    first_new = beta_one * first_old + (1.0 - beta_one) * projected
    second_new = beta_two * second_old + (1.0 - beta_two) * projected * projected
    my_rank = lax.dynamic_index_in_dim(rank, here, keepdims=False)
    keeping = (jnp.arange(rank_full, dtype=jnp.int32) < my_rank).astype(jnp.float32)[:, None]
    update = keeping * (first_new / bias_one) / (jnp.sqrt(second_new / bias_two) + epsilon)
    delta = (
        jnp.dot(old_basis, update.astype(jnp.bfloat16), preferred_element_type=jnp.float32)
        * inverse_root
    ).astype(jnp.bfloat16)
    back_delta = exchange(delta.reshape(owners, shard, quarter))
    full_delta = lax.all_gather(back_delta, "dp", axis=2, tiled=True)
    new_weight = (weight.astype(jnp.float32) - step_size * full_delta.astype(jnp.float32)).astype(
        jnp.bfloat16
    )

    spread = exchange(to_chunks(projected.astype(jnp.bfloat16)))
    spread = pick(source, spread).reshape(capacity, owners, 8, 128)
    spread = exchange(spread, axis=1)
    here_projected = from_chunks(spread, rank_full, quarter).astype(jnp.float32)
    matched = slots[:, None] == (here * capacity + jnp.arange(capacity, dtype=jnp.int32))[None, :]
    valid = jnp.any(matched, axis=0)[:, None, None]
    first_out = jnp.where(
        valid, beta_one * first_moment + (1.0 - beta_one) * here_projected, 0.0
    )
    second_out = jnp.where(
        valid,
        beta_two * second_moment + (1.0 - beta_two) * here_projected * here_projected,
        0.0,
    )

    sample = jnp.dot(whole, sketch, preferred_element_type=jnp.float32)
    gram = lax.dot_general(
        sample, sample, (((0,), (0,)), ((), ())), precision=lax.Precision.HIGHEST
    )
    inverse = inverse_factor(gram)
    solved = lax.dot_general(
        sample, inverse, (((1,), (1,)), ((), ())), precision=lax.Precision.HIGHEST
    )
    fresh = (solved * root).astype(jnp.bfloat16).reshape(owners, shard, rank_full)
    new_basis = exchange(fresh).astype(jnp.float32)
    return (new_weight, new_basis, first_out, second_out)


def solution(mesh):
    in_specs = (
        P("dp", None, "rows", None),
        P(None, "rows", None),
        P(None, "rows", None),
        P("rows", None, "dp"),
        P("rows", None, "dp"),
        P(),
        P(),
        P(),
    )
    out_specs = (
        P(None, "rows", None),
        P(None, "rows", None),
        P("rows", None, "dp"),
        P("rows", None, "dp"),
    )
    return jax.shard_map(
        per_device, mesh=mesh, in_specs=in_specs, out_specs=out_specs, check_vma=False
    )
```

time: 746 us -> 307 us (0.41)
  other arithmetic: 222 us -> 13 us
  waiting for transfers between devices: 334 us -> 134 us
  local copies, waits for them, and re-layouts: 72.4 us -> 12.9 us
  matrix products: 55.7 us -> 7.55 us
  Pallas kernels: 0 us -> 45.1 us
  blocking collectives: 0 us -> 23.5 us
  starting transfers between devices: 42 us -> 55.6 us
    another operation x14 -> x1, other arithmetic: 213 us -> 1.15 us  [per_device(): jnp.stack([to_chunks(first_moment.astype(jnp.bfloat16)), to_chunks(second...]
    all_to_all x4 -> x8, waiting for transfers between devices: 232 us -> 133 us  [the longest x7 111 us: exchange(): lax.all_to_all(data, 'rows', split_axis=axis, concat_axis=axis, tiled=True)]
    psum x1 -> x0, waiting for transfers between devices: 65.7 us -> none  [per_device(): total = lax.psum(grads[0], 'dp').astype(jnp.float32).astype(jnp.bfloat16)]
    pallas_call x0 -> x3, Pallas kernels: none -> 45.1 us  [the longest x1 40.2 us: inverse_factor(): pl.pallas_call(inverse_factor_kernel, out_shape=jax.ShapeDtypeStruct((siz...]
    dot_general x8 -> x5, matrix products: 45.1 us -> 7.55 us  [the longest x1 2.54 us: per_device(): lax.dot_general(sample, sample, (((0,), (0,)), ((), ())), precision=lax.P...]
    all_gather x1 -> x2, waiting for transfers between devices: 35.8 us -> 0.02 us  [the longest x1 0.02 us: per_device(): whole = lax.all_gather(own, 'dp', axis=1, tiled=True)]
    unnamed x26 -> x24, local copies, waits for them, and re-layouts: 28.4 us -> 1.94 us
    all_to_all x0 -> x1, blocking collectives: none -> 23.5 us  [exchange(): lax.all_to_all(data, 'rows', split_axis=axis, concat_axis=axis, tiled=True)]
  transfers between devices with their start and end apart: 6 -> 10, of which waited for: 4 -> 8; matrix products, arithmetic and copies ran while one was open for 39% -> 5% of each run, Pallas kernels for 0% -> 14%
where the time goes in v1:
time: 307 us; the launch traced here: 306 us
  waiting for transfers between devices  134 us (44%)
  starting transfers between devices  55.6 us (18%)
  Pallas kernels  45.1 us (15%)
  blocking collectives  23.5 us (8%)
  between operations  14.3 us (5%)
  other arithmetic  13 us (4%)
  local copies, waits for them, and re-layouts  12.9 us (4%)
  matrix products  7.55 us (2%)
    all_to_all x7, waiting for transfers between devices, exchange(): lax.all_to_all(data, 'rows', split_axis=axis, concat_axis=axis, tiled=True)  111 us
    all_to_all x7, starting transfers between devices, exchange(): lax.all_to_all(data, 'rows', split_axis=axis, concat_axis=axis, tiled=True)  50.5 us
    pallas_call x1, Pallas kernels, inverse_factor(): pl.pallas_call(inverse_factor_kernel, out_shape=jax.ShapeDtypeStruct((siz...  40.2 us
    all_to_all x1, blocking collectives, exchange(): lax.all_to_all(data, 'rows', split_axis=axis, concat_axis=axis, tiled=True)  23.5 us
    all_to_all x1, waiting for transfers between devices, per_device(): parts = lax.all_to_all(parts, 'dp', split_axis=0, concat_axis=0, tiled=True)  22.3 us
  transfers between devices with their start and end apart: 10, of which 8 were waited for; matrix products, arithmetic and copies ran while one was open for 5% of the time, Pallas kernels for 14%

profile of v1, /device:TPU:1, one launch (start us, length us, event | category | flops | bytes accessed | tf_op | source)
XLA Modules:
  0.0 305.8 jit_solution(15050064650460022140)
XLA Ops:
  7.2 3.4 %reshape_squeeze.2 = bf16[64,16,4,256]{3,2,1,0:T(4,128)(2,1)S(1)} reshape(bf16[1,64,16,1024]{3,2,1,0:T(8,128)(2,1)} %param.8) | data formatting | bytes 4194304 | tf_op jit(solution)/shard_map/reshape;squeeze | solution.py:147
  10.6 1.6 copy.50
  12.2 4.8 %all-to-all-start.2 = ((bf16[4,64,16,256]{3,2,1,0:T(8,128)(2,1)}), bf16[4,64,16,256]{3,2,1,0:T(8,128)(2,1)S(1)}, u32[]{:S(2)}, u32[]{:S(2)}) async-start(bf16[4,64,16,256]{3,2,1,0:T(8,128)(2,1)} %copy.50), calls=%async_computation.2 | async-start | bytes 4194304 | tf_op jit(solution)/shard_map/all_to_all | solution.py:148
  17.0 2.1 convert_element_type.78
  19.1 22.3 %all-to-all-done.2 = bf16[4,64,16,256]{3,2,1,0:T(8,128)(2,1)S(1)} async-done(((bf16[4,64,16,256]{3,2,1,0:T(8,128)(2,1)}), bf16[4,64,16,256]{3,2,1,0:T(8,128)(2,1)S(1)}, u32[]{:S(2)}, u32[]{:S(2)}) %all-to-all-start.2) | async-done | bytes 2097184 | tf_op jit(solution)/shard_map/all_to_all | solution.py:148
  41.4 14.6 %all-to-all-start.4 = ((bf16[64,16,256]{2,1,0:T(8,128)(2,1)}), bf16[64,16,256]{2,1,0:T(8,128)(2,1)S(1)}, u32[]{:S(2)}, u32[]{:S(2)}) async-start(bf16[64,16,256]{2,1,0:T(8,128)(2,1)} %convert_element_type.78), calls=%async_computation.4 | async-start | bytes 1048576 | tf_op jit(solution)/shard_map/all_to_all | solution.py:128
  56.0 1.2 reduce_sum.22
  57.2 16.1 %all-to-all-done.4 = bf16[64,16,256]{2,1,0:T(8,128)(2,1)S(1)} async-done(((bf16[64,16,256]{2,1,0:T(8,128)(2,1)}), bf16[64,16,256]{2,1,0:T(8,128)(2,1)S(1)}, u32[]{:S(2)}, u32[]{:S(2)}) %all-to-all-start.4) | async-done | bytes 524320 | tf_op jit(solution)/shard_map/all_to_all | solution.py:128
  73.3 6.3 %all-to-all-start.3 = ((bf16[64,16,256]{2,1,0:T(8,128)(2,1)}), bf16[64,16,256]{2,1,0:T(8,128)(2,1)S(1)}, u32[]{:S(2)}, u32[]{:S(2)}) async-start(bf16[64,16,256]{2,1,0:T(8,128)(2,1)} %reduce_sum.22), calls=%async_computation.3 | async-start | bytes 1048576 | tf_op jit(solution)/shard_map/all_to_all | solution.py:128
  79.6 0.2 convert_reduce_fusion
  79.8 17.1 %all-to-all-done.3 = bf16[64,16,256]{2,1,0:T(8,128)(2,1)S(1)} async-done(((bf16[64,16,256]{2,1,0:T(8,128)(2,1)}), bf16[64,16,256]{2,1,0:T(8,128)(2,1)S(1)}, u32[]{:S(2)}, u32[]{:S(2)}) %all-to-all-start.3) | async-done | bytes 524320 | tf_op jit(solution)/shard_map/all_to_all | solution.py:128
  96.9 0.3 convolution_bitcast_fusion
  97.3 0.4 copy-done.2
  97.7 0.8 copy.55
  98.5 6.3 %all-to-all-start.7 = ((bf16[64,8,128]{2,1,0:T(8,128)(2,1)}), bf16[64,8,128]{2,1,0:T(8,128)(2,1)S(1)}, u32[]{:S(2)}, u32[]{:S(2)}) async-start(bf16[64,8,128]{2,1,0:T(8,128)(2,1)} %bitcast.27), calls=%async_computation.7 | async-start | bytes 262144 | tf_op jit(solution)/shard_map/all_to_all | solution.py:128
  104.8 0.7 select_reduce_fusion.index_ref
  105.5 9.7 %all-to-all-done.7.data_ref = bf16[64,8,128]{2,1,0:T(8,128)(2,1)S(1)} async-done(((bf16[64,8,128]{2,1,0:T(8,128)(2,1)}), bf16[64,8,128]{2,1,0:T(8,128)(2,1)S(1)}, u32[]{:S(2)}, u32[]{:S(2)}) %all-to-all-start.7) | async-done | bytes 131104 | tf_op jit(solution)/shard_map/all_to_all | solution.py:128
  115.1 0.7 copy-done.6
  115.8 2.6 pick.3
  118.4 1.9 copy.56
  120.3 4.9 %all-to-all-start.8 = ((bf16[4,64,8,128]{3,2,0,1:T(8,128)(2,1)}), bf16[4,64,8,128]{3,2,0,1:T(8,128)(2,1)S(1)}, u32[]{:S(2)}, u32[]{:S(2)}) async-start(bf16[4,64,8,128]{3,2,0,1:T(8,128)(2,1)} %copy.56), calls=%async_computation.8 | async-start | bytes 1048576 | tf_op jit(solution)/shard_map/all_to_all | solution.py:128
  125.2 0.2 compare_reduce_fusion
  125.4 17.1 %all-to-all-done.8 = bf16[4,64,8,128]{3,2,0,1:T(8,128)(2,1)S(1)} async-done(((bf16[4,64,8,128]{3,2,0,1:T(8,128)(2,1)}), bf16[4,64,8,128]{3,2,0,1:T(8,128)(2,1)S(1)}, u32[]{:S(2)}, u32[]{:S(2)}) %all-to-all-start.8) | async-done | bytes 524320 | tf_op jit(solution)/shard_map/all_to_all | solution.py:128
  142.6 1.8 fusion.4
  144.5 0.1 copy.48
  144.6 1.1 pad_maximum_fusion
  145.8 6.3 %all-to-all-start = ((bf16[4,64,2,8,128]{4,3,2,0,1:T(8,128)(2,1)}), bf16[4,64,2,8,128]{4,3,2,0,1:T(8,128)(2,1)S(1)}, u32[]{:S(2)}, u32[]{:S(2)}) async-start(bf16[4,64,2,8,128]{4,3,2,0,1:T(8,128)(2,1)} %pad_maximum_fusion), calls=%async_computation | async-start | bytes 2097152 | tf_op jit(solution)/shard_map/all_to_all | solution.py:128
  152.1 0.7 all-gather.5.cloned.1.call-update
  152.8 27.8 %all-to-all-done = bf16[4,64,2,8,128]{4,3,2,0,1:T(8,128)(2,1)S(1)} async-done(((bf16[4,64,2,8,128]{4,3,2,0,1:T(8,128)(2,1)}), bf16[4,64,2,8,128]{4,3,2,0,1:T(8,128)(2,1)S(1)}, u32[]{:S(2)}, u32[]{:S(2)}) %all-to-all-start) | async-done | bytes 1048608 | tf_op jit(solution)/shard_map/all_to_all | solution.py:128
  180.6 1.1 copy.49
  181.8 2.2 pick.2
  184.0 6.2 %all-to-all-start.1 = ((bf16[64,16,128]{2,1,0:T(8,128)(2,1)}), bf16[64,16,128]{2,1,0:T(8,128)(2,1)S(1)}, u32[]{:S(2)}, u32[]{:S(2)}) async-start(bf16[64,16,128]{2,1,0:T(8,128)(2,1)} %pick.2), calls=%async_computation.1 | async-start | bytes 524288 | tf_op jit(solution)/shard_map/all_to_all | solution.py:128
  190.2 0.6 dynamic_slice.4
  190.8 0.6 compare_select_fusion
  191.5 10.7 %all-to-all-done.1 = bf16[64,16,128]{2,1,0:T(8,128)(2,1)S(1)} async-done(((bf16[64,16,128]{2,1,0:T(8,128)(2,1)}), bf16[64,16,128]{2,1,0:T(8,128)(2,1)S(1)}, u32[]{:S(2)}, u32[]{:S(2)}) %all-to-all-start.1) | async-done | bytes 262176 | tf_op jit(solution)/shard_map/all_to_all | solution.py:128
  202.6 0.4 fusion.2
  203.0 1.0 copy.54
  204.0 6.0 %all-to-all-start.5 = ((bf16[64,16,256]{2,1,0:T(8,128)(2,1)}), bf16[64,16,256]{2,1,0:T(8,128)(2,1)S(1)}, u32[]{:S(2)}, u32[]{:S(2)}) async-start(bf16[64,16,256]{2,1,0:T(8,128)(2,1)} %bitcast.21), calls=%async_computation.5 | async-start | bytes 1048576 | tf_op jit(solution)/shard_map/all_to_all | solution.py:128
  210.0 0.2 all-gather.3.cloned.1.call-start
  210.3 2.3 fusion.29
  212.6 2.5 fusion.30.gram_ref
  215.1 12.2 %all-to-all-done.5 = bf16[64,16,256]{2,1,0:T(8,128)(2,1)S(1)} async-done(((bf16[64,16,256]{2,1,0:T(8,128)(2,1)}), bf16[64,16,256]{2,1,0:T(8,128)(2,1)S(1)}, u32[]{:S(2)}, u32[]{:S(2)}) %all-to-all-start.5) | async-done | bytes 524320 | tf_op jit(solution)/shard_map/all_to_all | solution.py:128
  227.3 0.8 copy-done.3
  228.1 40.2 %inverse_factor.1 = f32[256,256]{1,0:T(8,128)} custom-call(f32[256,256]{1,0:T(8,128)} %fusion.30.gram_ref), custom_call_target="tpu_custom_call" | custom-call | flops 20000000000 | bytes 524288 | tf_op jit(solution)/shard_map/inverse_factor/pallas_call | solution.py:72
  268.4 2.0 fusion
  270.4 23.5 %all_to_all.45 = bf16[64,16,256]{2,1,0:T(8,128)(2,1)S(1)} all-to-all(bf16[64,16,256]{2,1,0:T(8,128)(2,1)S(1)} %bitcast.88), channel_id=1, replica_groups=mesh['dp'=4,'rows'=64] {'rows'}, dimensions={0} | all-to-all | bytes 1048576 | tf_op jit(solution)/shard_map/all_to_all | solution.py:128
  293.9 1.1 convert_element_type.86
  295.0 3.9 %subtract_convert_fusion = bf16[64,16,1024]{2,1,0:T(8,128)(2,1)} fusion(bf16[64,16,1024]{2,1,0:T(8,128)(2,1)} %all-gather.3.cloned.1.call-done, bf16[64,16,1024]{2,1,0:T(8,128)(2,1)S(1)} %copy-done.1), kind=kLoop, calls=%fused_computation | loop fusion | flops 5242880 | bytes 6291456 | tf_op jit(solution)/shard_map/convert_element_type | solution.py:186
  (32 shorter events, 0.6 us)
Async XLA Ops:
  7.2 203.1 %copy-start = (bf16[1024,256]{1,0:T(8,128)(2,1)S(1)}, bf16[1024,256]{1,0:T(8,128)(2,1)}, u32[]{:S(2)}) copy-start(bf16[1024,256]{1,0:T(8,128)(2,1)} %param.13) | copy-start | bytes 1572868
  12.2 29.2 %all-to-all-start.2 = ((bf16[4,64,16,256]{3,2,1,0:T(8,128)(2,1)}), bf16[4,64,16,256]{3,2,1,0:T(8,128)(2,1)S(1)}, u32[]{:S(2)}, u32[]{:S(2)}) async-start(bf16[4,64,16,256]{3,2,1,0:T(8,128)(2,1)} %copy.50), calls=%async_computation.2 | async-start | bytes 4194304 | tf_op jit(solution)/shard_map/all_to_all | solution.py:148
  41.4 31.9 %all-to-all-start.4 = ((bf16[64,16,256]{2,1,0:T(8,128)(2,1)}), bf16[64,16,256]{2,1,0:T(8,128)(2,1)S(1)}, u32[]{:S(2)}, u32[]{:S(2)}) async-start(bf16[64,16,256]{2,1,0:T(8,128)(2,1)} %convert_element_type.78), calls=%async_computation.4 | async-start | bytes 1048576 | tf_op jit(solution)/shard_map/all_to_all | solution.py:128
  56.0 23.6 %copy-start.10 = (s32[64]{0:T(128)S(1)}, s32[64]{0:T(128)}, u32[]{:S(2)}) copy-start(s32[64]{0:T(128)} %param.14) | copy-start | bytes 772
  73.3 23.6 %copy-start.7 = (bf16[64,16,256]{2,1,0:T(8,128)(2,1)}, bf16[64,16,256]{2,1,0:T(8,128)(2,1)S(1)}, u32[]{:S(2)}) copy-start(bf16[64,16,256]{2,1,0:T(8,128)(2,1)S(1)} %all-to-all-done.4) | copy-start | bytes 1572868
  73.3 23.6 %all-to-all-start.3 = ((bf16[64,16,256]{2,1,0:T(8,128)(2,1)}), bf16[64,16,256]{2,1,0:T(8,128)(2,1)S(1)}, u32[]{:S(2)}, u32[]{:S(2)}) async-start(bf16[64,16,256]{2,1,0:T(8,128)(2,1)} %reduce_sum.22), calls=%async_computation.3 | async-start | bytes 1048576 | tf_op jit(solution)/shard_map/all_to_all | solution.py:128
  96.9 0.8 copy-start.2
  97.7 44.8 %copy-start.4 = (f32[4,256,256]{2,1,0:T(8,128)S(1)}, f32[4,256,256]{2,1,0:T(8,128)}, u32[]{:S(2)}) copy-start(f32[4,256,256]{2,1,0:T(8,128)} %param.12) | copy-start | bytes 3145732
  97.7 44.8 %copy-start.5 = (f32[4,256,256]{2,1,0:T(8,128)S(1)}, f32[4,256,256]{2,1,0:T(8,128)}, u32[]{:S(2)}) copy-start(f32[4,256,256]{2,1,0:T(8,128)} %param.11) | copy-start | bytes 3145732
  98.5 16.6 %all-to-all-start.7 = ((bf16[64,8,128]{2,1,0:T(8,128)(2,1)}), bf16[64,8,128]{2,1,0:T(8,128)(2,1)S(1)}, u32[]{:S(2)}, u32[]{:S(2)}) async-start(bf16[64,8,128]{2,1,0:T(8,128)(2,1)} %bitcast.27), calls=%async_computation.7 | async-start | bytes 262144 | tf_op jit(solution)/shard_map/all_to_all | solution.py:128
  104.8 39.6 %copy-start.9 = (s32[64]{0:T(128)}, s32[64]{0:T(128)S(1)}, u32[]{:S(2)}) copy-start(s32[64]{0:T(128)S(1)} %get-tuple-element.4.index_ref) | copy-start | bytes 772
  115.1 0.7 copy-start.6
  120.3 22.2 %all-to-all-start.8 = ((bf16[4,64,8,128]{3,2,0,1:T(8,128)(2,1)}), bf16[4,64,8,128]{3,2,0,1:T(8,128)(2,1)S(1)}, u32[]{:S(2)}, u32[]{:S(2)}) async-start(bf16[4,64,8,128]{3,2,0,1:T(8,128)(2,1)} %copy.56), calls=%async_computation.8 | async-start | bytes 1048576 | tf_op jit(solution)/shard_map/all_to_all | solution.py:128
  145.8 34.8 %all-to-all-start = ((bf16[4,64,2,8,128]{4,3,2,0,1:T(8,128)(2,1)}), bf16[4,64,2,8,128]{4,3,2,0,1:T(8,128)(2,1)S(1)}, u32[]{:S(2)}, u32[]{:S(2)}) async-start(bf16[4,64,2,8,128]{4,3,2,0,1:T(8,128)(2,1)} %pad_maximum_fusion), calls=%async_computation | async-start | bytes 2097152 | tf_op jit(solution)/shard_map/all_to_all | solution.py:128
  152.1 58.2 %all-gather.5.cloned.1.call-start = ((), (), s32[]{:S(2)}) async-start(), calls=%async_computation.10 | async-start | bytes 2621440 | tf_op jit(solution)/shard_map/all_gather | solution.py:167
  152.8 37.4 %copy-start.11 = (s32[64]{0:T(128)S(1)}, s32[64]{0:T(128)}, u32[]{:S(2)}) copy-start(s32[64]{0:T(128)} %param.15) | copy-start | bytes 772
  181.8 20.8 %copy-start.8 = (bf16[64,16,256]{2,1,0:T(8,128)(2,1)S(1)}, bf16[64,16,256]{2,1,0:T(8,128)(2,1)}, u32[]{:S(2)}) copy-start(bf16[64,16,256]{2,1,0:T(8,128)(2,1)} %copy-done.7) | copy-start | bytes 1572868
  184.0 18.2 %all-to-all-start.1 = ((bf16[64,16,128]{2,1,0:T(8,128)(2,1)}), bf16[64,16,128]{2,1,0:T(8,128)(2,1)S(1)}, u32[]{:S(2)}, u32[]{:S(2)}) async-start(bf16[64,16,128]{2,1,0:T(8,128)(2,1)} %pick.2), calls=%async_computation.1 | async-start | bytes 524288 | tf_op jit(solution)/shard_map/all_to_all | solution.py:128
  204.0 23.4 %all-to-all-start.5 = ((bf16[64,16,256]{2,1,0:T(8,128)(2,1)}), bf16[64,16,256]{2,1,0:T(8,128)(2,1)S(1)}, u32[]{:S(2)}, u32[]{:S(2)}) async-start(bf16[64,16,256]{2,1,0:T(8,128)(2,1)} %bitcast.21), calls=%async_computation.5 | async-start | bytes 1048576 | tf_op jit(solution)/shard_map/all_to_all | solution.py:128
  210.0 85.0 %all-gather.3.cloned.1.call-start = ((), (), s32[]{:S(2)}) async-start(), calls=%async_computation.9 | async-start | bytes 2621440 | tf_op jit(solution)/shard_map/all_gather | solution.py:185
  227.3 0.8 copy-start.3
  270.4 24.7 %copy-start.1 = (bf16[64,16,1024]{2,1,0:T(8,128)(2,1)S(1)}, bf16[64,16,1024]{2,1,0:T(8,128)(2,1)}, u32[]{:S(2)}) copy-start(bf16[64,16,1024]{2,1,0:T(8,128)(2,1)} %param.9) | copy-start | bytes 6291460
Sparse Core Ops, SparseCore 0:
  154.7 35.2 all-gather.4
  228.3 31.4 all-gather.2

commit v2 on v1

--- a/solution.py
+++ b/solution.py
@@ -138,17 +138,11 @@
     root = float(total_rows) ** 0.5
     inverse_root = float(total_rows) ** (-0.5)
     slots = slot_of(owner, capacity)
-    column = slots % capacity * owners + slots // capacity
-    column_ids = jnp.arange(capacity * owners, dtype=jnp.int32)
-    hit = column[:, None] == column_ids[None, :]
+    slot_ids = jnp.arange(capacity * owners, dtype=jnp.int32)
+    hit = slots[:, None] == slot_ids[None, :]
     matrix_ids = jnp.arange(count, dtype=jnp.int32)
     source = jnp.max(jnp.where(hit, matrix_ids[:, None], -1), axis=0)
-
-    parts = jnp.transpose(grads[0].reshape(count, shard, groups, quarter), (2, 0, 1, 3))
-    parts = lax.all_to_all(parts, "dp", split_axis=0, concat_axis=0, tiled=True)
-    mine = jnp.sum(parts.astype(jnp.float32), axis=0).astype(jnp.bfloat16)
-
-    old_basis = exchange(basis.astype(jnp.bfloat16)).reshape(total_rows, rank_full)
+    pieces = shard * quarter // 1024
 
     moments = jnp.stack(
         [
@@ -157,13 +151,22 @@
         ],
         axis=2,
     )
-    moments = exchange(moments, axis=1)
-    moments = pick(column, moments.reshape(capacity * owners, 16, 128))
-    moments = exchange(moments).reshape(owners, 2, 8, 128)
-    first_old = from_chunks(moments[:, 0], rank_full, quarter).astype(jnp.float32)
-    second_old = from_chunks(moments[:, 1], rank_full, quarter).astype(jnp.float32)
-
-    own = exchange(mine).reshape(total_rows, quarter)
+    moments = jnp.transpose(moments, (1, 0, 2, 3, 4)).reshape(owners, 2 * capacity, 8, 128)
+    first_trip = jnp.concatenate([moments, to_chunks(basis.astype(jnp.bfloat16))], axis=1)
+    first_trip = exchange(first_trip)
+    moments = first_trip[:, : 2 * capacity].reshape(owners * capacity, 16, 128)
+    old_basis = from_chunks(first_trip[:, 2 * capacity :], shard, rank_full)
+    old_basis = old_basis.reshape(total_rows, rank_full)
+    moments = pick(slots, moments).reshape(count, 2, 8, 128)
+
+    parts = jnp.transpose(grads[0].reshape(count, shard, groups, quarter), (2, 0, 1, 3))
+    parts = lax.all_to_all(parts, "dp", split_axis=0, concat_axis=0, tiled=True)
+    mine = jnp.sum(parts.astype(jnp.float32), axis=0).astype(jnp.bfloat16)
+
+    second_trip = exchange(jnp.concatenate([to_chunks(mine), moments], axis=1))
+    own = from_chunks(second_trip[:, :pieces], shard, quarter).reshape(total_rows, quarter)
+    first_old = from_chunks(second_trip[:, pieces], rank_full, quarter).astype(jnp.float32)
+    second_old = from_chunks(second_trip[:, pieces + 1], rank_full, quarter).astype(jnp.float32)
     whole = lax.all_gather(own, "dp", axis=1, tiled=True)
 
     projected = (
@@ -181,15 +184,24 @@
         jnp.dot(old_basis, update.astype(jnp.bfloat16), preferred_element_type=jnp.float32)
         * inverse_root
     ).astype(jnp.bfloat16)
-    back_delta = exchange(delta.reshape(owners, shard, quarter))
+
+    third_trip = exchange(
+        jnp.concatenate(
+            [
+                to_chunks(delta.reshape(owners, shard, quarter)),
+                to_chunks(projected.astype(jnp.bfloat16))[:, None],
+            ],
+            axis=1,
+        )
+    )
+    back_delta = from_chunks(third_trip[:, :pieces], shard, quarter)
     full_delta = lax.all_gather(back_delta, "dp", axis=2, tiled=True)
     new_weight = (weight.astype(jnp.float32) - step_size * full_delta.astype(jnp.float32)).astype(
         jnp.bfloat16
     )
 
-    spread = exchange(to_chunks(projected.astype(jnp.bfloat16)))
-    spread = pick(source, spread).reshape(capacity, owners, 8, 128)
-    spread = exchange(spread, axis=1)
+    spread = pick(source, third_trip[:, pieces]).reshape(owners, capacity, 8, 128)
+    spread = jnp.transpose(exchange(spread), (1, 0, 2, 3))
     here_projected = from_chunks(spread, rank_full, quarter).astype(jnp.float32)
     matched = slots[:, None] == (here * capacity + jnp.arange(capacity, dtype=jnp.int32))[None, :]
     valid = jnp.any(matched, axis=0)[:, None, None]

time: 307 us -> 263 us (0.86)
  waiting for transfers between devices: 134 us -> 93 us
  starting transfers between devices: 55.6 us -> 42.9 us
  blocking collectives: 23.5 us -> 28.9 us
  other arithmetic: 13 us -> 17.6 us
    all_to_all x7 -> x4, waiting for transfers between devices: 111 us -> 72.9 us  [exchange(): lax.all_to_all(data, 'rows', split_axis=axis, concat_axis=axis, tiled=True)]
    all_to_all x7 -> x4, starting transfers between devices: 50.5 us -> 38 us  [exchange(): lax.all_to_all(data, 'rows', split_axis=axis, concat_axis=axis, tiled=True)]
    all_to_all x1, blocking collectives: 23.5 us -> 28.9 us  [exchange(): lax.all_to_all(data, 'rows', split_axis=axis, concat_axis=axis, tiled=True)]
    slice x0 -> x4, local copies, waits for them, and re-layouts: none -> 5.02 us  [the longest x1 2.27 us: per_device(): moments = first_trip[:, :2 * capacity].reshape(owners * capacity, 16, 128)]
    concatenate x0 -> x3, other arithmetic: none -> 3.21 us  [the longest x1 1.28 us: per_device(): jnp.concatenate([moments, to_chunks(basis.astype(jnp.bfloat16))], axis=1)]
  transfers between devices with their start and end apart: 10 -> 7, of which waited for: 8 -> 4; matrix products, arithmetic and copies ran while one was open for 5% -> 9% of each run, Pallas kernels for 14% -> 16%
where the time goes in v2:
time: 263 us; the launch traced here: 262 us
  waiting for transfers between devices  93 us (35%)
  Pallas kernels  45 us (17%)
  starting transfers between devices  42.9 us (16%)
  blocking collectives  28.9 us (11%)
  other arithmetic  17.6 us (7%)
  between operations  14.3 us (5%)
  local copies, waits for them, and re-layouts  11.6 us (4%)
  matrix products  8.48 us (3%)
    all_to_all x4, waiting for transfers between devices, exchange(): lax.all_to_all(data, 'rows', split_axis=axis, concat_axis=axis, tiled=True)  72.9 us
    pallas_call x1, Pallas kernels, inverse_factor(): pl.pallas_call(inverse_factor_kernel, out_shape=jax.ShapeDtypeStruct((siz...  40.2 us
    all_to_all x4, starting transfers between devices, exchange(): lax.all_to_all(data, 'rows', split_axis=axis, concat_axis=axis, tiled=True)  38 us
    all_to_all x1, blocking collectives, exchange(): lax.all_to_all(data, 'rows', split_axis=axis, concat_axis=axis, tiled=True)  28.9 us
    all_to_all x1, waiting for transfers between devices, per_device(): parts = lax.all_to_all(parts, 'dp', split_axis=0, concat_axis=0, tiled=True)  20 us
  transfers between devices with their start and end apart: 7, of which 4 were waited for; matrix products, arithmetic and copies ran while one was open for 9% of the time, Pallas kernels for 16%

profile of v2, /device:TPU:1, one launch (start us, length us, event | category | flops | bytes accessed | tf_op | source)
XLA Modules:
  0.0 261.8 jit_solution(17137955813099103976)
XLA Ops:
  7.2 3.4 %reshape_squeeze.2 = bf16[64,16,4,256]{3,2,1,0:T(4,128)(2,1)S(1)} reshape(bf16[1,64,16,1024]{3,2,1,0:T(8,128)(2,1)} %param.8) | data formatting | bytes 4194304 | tf_op jit(solution)/shard_map/reshape;squeeze | solution.py:162
  10.6 1.6 copy.34
  12.2 4.8 %all-to-all-start.1 = ((bf16[4,64,16,256]{3,2,1,0:T(8,128)(2,1)}), bf16[4,64,16,256]{3,2,1,0:T(8,128)(2,1)S(1)}, u32[]{:S(2)}, u32[]{:S(2)}) async-start(bf16[4,64,16,256]{3,2,1,0:T(8,128)(2,1)} %copy.34), calls=%async_computation.1 | async-start | bytes 4194304 | tf_op jit(solution)/shard_map/all_to_all | solution.py:163
  17.0 1.4 convert_element_type.73
  18.4 1.3 convert_element_type.71
  19.7 0.1 convert_element_type.72
  19.8 0.1 pad_maximum_fusion.1
  19.9 0.3 copy.37
  20.2 1.3 pad_maximum_fusion
  21.4 20.0 %all-to-all-done.1 = bf16[4,64,16,256]{3,2,1,0:T(8,128)(2,1)S(1)} async-done(((bf16[4,64,16,256]{3,2,1,0:T(8,128)(2,1)}), bf16[4,64,16,256]{3,2,1,0:T(8,128)(2,1)S(1)}, u32[]{:S(2)}, u32[]{:S(2)}) %all-to-all-start.1) | async-done | bytes 2097184 | tf_op jit(solution)/shard_map/all_to_all | solution.py:163
  41.4 14.7 %all-to-all-start = ((bf16[64,12,8,128]{3,2,1,0:T(8,128)(2,1)}), bf16[64,12,8,128]{3,2,1,0:T(8,128)(2,1)}, u32[]{:S(2)}, u32[]{:S(2)}) async-start(bf16[64,12,8,128]{3,2,1,0:T(8,128)(2,1)} %pad_maximum_fusion), calls=%async_computation | async-start | bytes 3145728 | tf_op jit(solution)/shard_map/all_to_all | solution.py:128
  56.1 0.0 all-gather.5.cloned.1.call-start
  56.2 0.2 convert_reduce_fusion
  56.4 0.5 multiply_add_fusion.index_ref
  56.9 0.6 reduce_sum.21
  57.5 38.3 %all-to-all-done = bf16[64,12,8,128]{3,2,1,0:T(8,128)(2,1)} async-done(((bf16[64,12,8,128]{3,2,1,0:T(8,128)(2,1)}), bf16[64,12,8,128]{3,2,1,0:T(8,128)(2,1)}, u32[]{:S(2)}, u32[]{:S(2)}) %all-to-all-start) | async-done | bytes 1572896 | tf_op jit(solution)/shard_map/all_to_all | solution.py:128
  95.9 2.3 slice.29
  98.1 2.2 pick.2
  100.3 1.0 pad_maximum_fusion.2
  101.4 28.9 %all_to_all.30 = bf16[64,6,8,128]{3,2,1,0:T(8,128)(2,1)S(1)} all-to-all(bf16[64,6,8,128]{3,2,1,0:T(8,128)(2,1)S(1)} %pad_maximum_fusion.2), channel_id=1, replica_groups=mesh['dp'=4,'rows'=64] {'rows'}, dimensions={0} | all-to-all | bytes 1572864 | tf_op jit(solution)/shard_map/all_to_all | solution.py:128
  130.3 0.8 slice.31
  131.1 0.0 all-gather.5.cloned.1.call-update
  131.1 0.6 dynamic_slice.4
  131.7 0.6 compare_select_fusion
  132.4 1.1 slice.28
  133.5 0.3 multiply_convert_fusion
  133.9 0.4 fusion.1
  134.3 0.9 pad_maximum_fusion.3
  135.2 6.2 %all-to-all-start.3 = ((bf16[64,5,8,128]{3,2,1,0:T(8,128)(2,1)}), bf16[64,5,8,128]{3,2,1,0:T(8,128)(2,1)S(1)}, u32[]{:S(2)}, u32[]{:S(2)}) async-start(bf16[64,5,8,128]{3,2,1,0:T(8,128)(2,1)} %pad_maximum_fusion.3), calls=%async_computation.3 | async-start | bytes 1310720 | tf_op jit(solution)/shard_map/all_to_all | solution.py:128
  141.4 0.7 select_reduce_fusion.index_ref
  142.1 19.5 %all-to-all-done.3 = bf16[64,5,8,128]{3,2,1,0:T(8,128)(2,1)S(1)} async-done(((bf16[64,5,8,128]{3,2,1,0:T(8,128)(2,1)}), bf16[64,5,8,128]{3,2,1,0:T(8,128)(2,1)S(1)}, u32[]{:S(2)}, u32[]{:S(2)}) %all-to-all-start.3) | async-done | bytes 655392 | tf_op jit(solution)/shard_map/all_to_all | solution.py:128
  161.5 0.7 slice_bitcast_fusion.data_ref
  162.2 2.6 pick.3
  164.8 6.3 %all-to-all-start.5 = ((bf16[64,4,8,128]{3,2,1,0:T(8,128)(2,1)}), bf16[64,4,8,128]{3,2,1,0:T(8,128)(2,1)S(1)}, u32[]{:S(2)}, u32[]{:S(2)}) async-start(bf16[64,4,8,128]{3,2,1,0:T(8,128)(2,1)} %bitcast.98), calls=%async_computation.5 | async-start | bytes 1048576 | tf_op jit(solution)/shard_map/all_to_all | solution.py:128
  171.1 0.0 all-gather.3.cloned.1.call-start
  171.1 0.8 slice.33
  172.0 0.0 all-gather.5.cloned.1.call-done
  172.0 2.3 fusion.18
  174.3 2.5 fusion.19.gram_ref
  176.9 40.2 %inverse_factor.1 = f32[256,256]{1,0:T(8,128)} custom-call(f32[256,256]{1,0:T(8,128)} %fusion.19.gram_ref), custom_call_target="tpu_custom_call" | custom-call | flops 20000000000 | bytes 524288 | tf_op jit(solution)/shard_map/inverse_factor/pallas_call | solution.py:72
  217.1 2.9 %fusion = bf16[1024,256]{1,0:T(8,128)(2,1)} fusion(f32[1024,256]{1,0:T(8,128)S(1)} %fusion.18, f32[256,256]{1,0:T(8,128)} %inverse_factor.1), kind=kOutput, calls=%fused_computation.5 | convolution fusion | flops 805830656 | bytes 1835008 | tf_op jit(solution)/shard_map/dot_general | solution.py:222
  220.0 10.8 %all-to-all-start.4 = ((bf16[64,16,256]{2,1,0:T(8,128)(2,1)}), bf16[64,16,256]{2,1,0:T(8,128)(2,1)}, u32[]{:S(2)}, u32[]{:S(2)}) async-start(bf16[64,16,256]{2,1,0:T(8,128)(2,1)} %bitcast.97), calls=%async_computation.4 | async-start | bytes 1048576 | tf_op jit(solution)/shard_map/all_to_all | solution.py:128
  230.8 0.2 compare_reduce_fusion
  231.0 0.1 convert_element_type.92
  231.2 1.7 fusion.3
  232.9 15.2 %all-to-all-done.4 = bf16[64,16,256]{2,1,0:T(8,128)(2,1)} async-done(((bf16[64,16,256]{2,1,0:T(8,128)(2,1)}), bf16[64,16,256]{2,1,0:T(8,128)(2,1)}, u32[]{:S(2)}, u32[]{:S(2)}) %all-to-all-start.4) | async-done | bytes 524320 | tf_op jit(solution)/shard_map/all_to_all | solution.py:128
  248.1 2.2 convert_element_type.83
  250.2 4.7 %subtract_convert_fusion = bf16[64,16,1024]{2,1,0:T(8,128)(2,1)} fusion(bf16[64,16,1024]{2,1,0:T(8,128)(2,1)} %all-gather.3.cloned.1.call-done, bf16[64,16,1024]{2,1,0:T(8,128)(2,1)} %param.9), kind=kLoop, calls=%fused_computation | loop fusion | flops 5242880 | bytes 6291456 | tf_op jit(solution)/shard_map/convert_element_type | solution.py:199
  (21 shorter events, 0.1 us)
Async XLA Ops:
  7.2 164.9 %copy-start = (bf16[1024,256]{1,0:T(8,128)(2,1)S(1)}, bf16[1024,256]{1,0:T(8,128)(2,1)}, u32[]{:S(2)}) copy-start(bf16[1024,256]{1,0:T(8,128)(2,1)} %param.13) | copy-start | bytes 1572868
  12.2 29.2 %all-to-all-start.1 = ((bf16[4,64,16,256]{3,2,1,0:T(8,128)(2,1)}), bf16[4,64,16,256]{3,2,1,0:T(8,128)(2,1)S(1)}, u32[]{:S(2)}, u32[]{:S(2)}) async-start(bf16[4,64,16,256]{3,2,1,0:T(8,128)(2,1)} %copy.34), calls=%async_computation.1 | async-start | bytes 4194304 | tf_op jit(solution)/shard_map/all_to_all | solution.py:163
  17.0 2.7 %copy-start.2 = (f32[4,256,256]{2,1,0:T(8,128)S(1)}, f32[4,256,256]{2,1,0:T(8,128)}, u32[]{:S(2)}) copy-start(f32[4,256,256]{2,1,0:T(8,128)} %param.12) | copy-start | bytes 3145732
  21.4 34.7 %copy-start.6 = (s32[64]{0:T(128)S(1)}, s32[64]{0:T(128)}, u32[]{:S(2)}) copy-start(s32[64]{0:T(128)} %param.14) | copy-start | bytes 772
  41.4 54.5 %all-to-all-start = ((bf16[64,12,8,128]{3,2,1,0:T(8,128)(2,1)}), bf16[64,12,8,128]{3,2,1,0:T(8,128)(2,1)}, u32[]{:S(2)}, u32[]{:S(2)}) async-start(bf16[64,12,8,128]{3,2,1,0:T(8,128)(2,1)} %pad_maximum_fusion), calls=%async_computation | async-start | bytes 3145728 | tf_op jit(solution)/shard_map/all_to_all | solution.py:128
  56.1 115.9 %all-gather.5.cloned.1.call-start = ((), (), s32[]{:S(2)}) async-start(), calls=%async_computation.7 | async-start | bytes 2621440 | tf_op jit(solution)/shard_map/all_gather | solution.py:170
  100.3 30.8 %copy-start.7 = (s32[64]{0:T(128)S(1)}, s32[64]{0:T(128)}, u32[]{:S(2)}) copy-start(s32[64]{0:T(128)} %param.15) | copy-start | bytes 772
  131.1 2.4 copy-start.1
  133.9 7.6 %copy-start.5 = (s32[64]{0:T(128)S(1)}, s32[64]{0:T(128)}, u32[]{:S(2)}) copy-start(s32[64]{0:T(128)} %multiply_add_fusion.index_ref) | copy-start | bytes 772
  135.2 26.3 %all-to-all-start.3 = ((bf16[64,5,8,128]{3,2,1,0:T(8,128)(2,1)}), bf16[64,5,8,128]{3,2,1,0:T(8,128)(2,1)S(1)}, u32[]{:S(2)}, u32[]{:S(2)}) async-start(bf16[64,5,8,128]{3,2,1,0:T(8,128)(2,1)} %pad_maximum_fusion.3), calls=%async_computation.3 | async-start | bytes 1310720 | tf_op jit(solution)/shard_map/all_to_all | solution.py:128
  164.8 55.2 %all-to-all-start.5 = ((bf16[64,4,8,128]{3,2,1,0:T(8,128)(2,1)}), bf16[64,4,8,128]{3,2,1,0:T(8,128)(2,1)S(1)}, u32[]{:S(2)}, u32[]{:S(2)}) async-start(bf16[64,4,8,128]{3,2,1,0:T(8,128)(2,1)} %bitcast.98), calls=%async_computation.5 | async-start | bytes 1048576 | tf_op jit(solution)/shard_map/all_to_all | solution.py:128
  171.1 79.1 %all-gather.3.cloned.1.call-start = ((), (), s32[]{:S(2)}) async-start(), calls=%async_computation.6 | async-start | bytes 2621440 | tf_op jit(solution)/shard_map/all_gather | solution.py:198
  217.1 14.0 %copy-start.3 = (f32[4,256,256]{2,1,0:T(8,128)S(1)}, f32[4,256,256]{2,1,0:T(8,128)}, u32[]{:S(2)}) copy-start(f32[4,256,256]{2,1,0:T(8,128)} %param.12) | copy-start | bytes 3145732
  220.0 11.2 %copy-start.4 = (f32[4,256,256]{2,1,0:T(8,128)S(1)}, f32[4,256,256]{2,1,0:T(8,128)}, u32[]{:S(2)}) copy-start(f32[4,256,256]{2,1,0:T(8,128)} %param.11) | copy-start | bytes 3145732
  220.0 28.1 %all-to-all-start.4 = ((bf16[64,16,256]{2,1,0:T(8,128)(2,1)}), bf16[64,16,256]{2,1,0:T(8,128)(2,1)}, u32[]{:S(2)}, u32[]{:S(2)}) async-start(bf16[64,16,256]{2,1,0:T(8,128)(2,1)} %bitcast.97), calls=%async_computation.4 | async-start | bytes 1048576 | tf_op jit(solution)/shard_map/all_to_all | solution.py:128
Sparse Core Ops, SparseCore 0:
  131.2 31.1 all-gather.4
  174.3 36.2 all-gather.2

commit v3 on v2

--- a/solution.py
+++ b/solution.py
@@ -12,7 +12,8 @@
 step_size = 0.5
 epsilon = 1e-08
 
-PANEL = 32
+PANEL = 64
+BLOCK = 8
 
 
 def slot_of(owner, capacity):
@@ -30,23 +31,56 @@
     row = lax.broadcasted_iota(jnp.int32, (size, size), 0)
     col = lax.broadcasted_iota(jnp.int32, (size, size), 1)
     work_ref[:, size:] = jnp.where(row == col, 1.0, 0.0)
-    lane = lax.broadcasted_iota(jnp.int32, (PANEL, 128), 1)
-    below = lax.broadcasted_iota(jnp.int32, (PANEL, 128), 0)
-    unit = jnp.where(lane == below + PANEL, 1.0, 0.0)
+    lane = lax.broadcasted_iota(jnp.int32, (8, 128), 1)
+    below = lax.broadcasted_iota(jnp.int32, (8, 128), 0)
     wide_lane = lax.broadcasted_iota(jnp.int32, (PANEL, size), 1)
+    tiles = PANEL // 8
+
+    def spread(line):
+        return jnp.broadcast_to(line, (8, 128))
 
     def panel(step, carry):
         head = work_ref[:PANEL, :]
-        aug = jnp.where(lane < PANEL, head[:, :128], unit)
-        scale = jnp.zeros((PANEL, 128), jnp.float32)
-        for j in range(PANEL):
-            pivot_row = aug[j : j + 1, :]
-            column = jnp.broadcast_to(aug[:, j : j + 1], (PANEL, 128))
-            pivot = column[j : j + 1, :]
-            factor = jnp.where(below > j, column / pivot, 0.0)
-            scale = jnp.where(below == j, lax.rsqrt(pivot), scale)
-            aug = aug - factor * pivot_row
-        inverse = (aug * scale)[:, PANEL : 2 * PANEL]
+        aug = []
+        for t in range(tiles):
+            unit = jnp.where(lane == below + (PANEL + 8 * t), 1.0, 0.0)
+            aug.append(jnp.where(lane < PANEL, head[8 * t : 8 * t + 8, :128], unit))
+        scale = [jnp.zeros((8, 128), jnp.float32) for _ in range(tiles)]
+        for j in range(0, PANEL, BLOCK):
+            block = range(BLOCK)
+            first = j // 8
+            cols = [
+                {t: spread(aug[t][:, j + k : j + k + 1]) for t in range(first, tiles)}
+                for k in block
+            ]
+            rows = []
+            small = []
+            for a in block:
+                t, s = divmod(j + a, 8)
+                rows.append(spread(aug[t][s : s + 1, :]))
+                small.append([spread(cols[c][t][s : s + 1, :]) for c in range(a + 1)])
+            recip = []
+            for k in block:
+                t, s = divmod(j + k, 8)
+                recip.append(1.0 / small[k][k])
+                scale[t] = jnp.where(below == s, lax.rsqrt(small[k][k]), scale[t])
+                for a in range(k + 1, BLOCK):
+                    ratio = small[a][k] * recip[k]
+                    rows[a] = rows[a] - ratio * rows[k]
+                    for c in range(k + 1, a + 1):
+                        small[a][c] = small[a][c] - ratio * small[c][k]
+            for t in range(first, tiles):
+                for k in block:
+                    if 8 * t + 7 <= j + k:
+                        continue
+                    factor = cols[k][t] * recip[k]
+                    for c in range(k + 1, BLOCK):
+                        cols[c][t] = cols[c][t] - factor * small[c][k]
+                    if 8 * t <= j + k:
+                        factor = jnp.where(below > j + k - 8 * t, factor, 0.0)
+                    aug[t] = aug[t] - factor * rows[k]
+        inverse = jnp.concatenate([x * y for x, y in zip(aug, scale)], axis=0)
+        inverse = inverse[:, PANEL : 2 * PANEL]
         solved = jnp.dot(
             inverse, head, precision=lax.Precision.HIGHEST, preferred_element_type=jnp.float32
         )
@@ -80,6 +114,80 @@
         ),
         name="inverse_factor",
     )(gram)
+
+
+def sum_kernel(grads_ref, out_ref, held_ref, local_sem, send_sem, recv_sem):
+    groups = held_ref.shape[0]
+    quarter = held_ref.shape[3]
+    me = lax.axis_index("dp")
+    barrier = pltpu.get_barrier_semaphore()
+    for d in range(1, groups):
+        pl.semaphore_signal(
+            barrier,
+            inc=1,
+            device_id={"dp": lax.rem(me + d, groups)},
+            device_id_type=pl.DeviceIdType.MESH,
+        )
+    pl.semaphore_wait(barrier, groups - 1)
+
+    def columns(who):
+        return grads_ref.at[0, :, :, pl.ds(pl.multiple_of(who * quarter, quarter), quarter)]
+
+    copies = []
+    for d in range(1, groups):
+        peer = lax.rem(me + d, groups)
+        copy = pltpu.make_async_remote_copy(
+            src_ref=columns(peer),
+            dst_ref=held_ref.at[d],
+            send_sem=send_sem.at[d - 1],
+            recv_sem=recv_sem.at[d - 1],
+            device_id={"dp": peer},
+            device_id_type=pl.DeviceIdType.MESH,
+        )
+        copy.start()
+        copies.append(copy)
+    own = pltpu.make_async_copy(columns(me), held_ref.at[0], local_sem)
+    own.start()
+    own.wait()
+    for copy in copies:
+        copy.wait()
+    step = 4
+
+    def add(i, carry):
+        at = pl.ds(i * step, step)
+        total = held_ref[0, at].astype(jnp.float32)
+        for d in range(1, groups):
+            total = total + held_ref[d, at].astype(jnp.float32)
+        for r in range(held_ref.shape[2] // 8):
+            for c in range(quarter // 128):
+                piece = total[:, 8 * r : 8 * r + 8, 128 * c : 128 * c + 128]
+                out_ref[at, r * (quarter // 128) + c] = piece.astype(jnp.bfloat16)
+        return carry
+
+    lax.fori_loop(0, held_ref.shape[1] // step, add, 0)
+
+
+def sum_quarters(grads, groups):
+    _, count, shard, width = grads.shape
+    quarter = width // groups
+    pieces = shard * quarter // 1024
+    return pl.pallas_call(
+        sum_kernel,
+        out_shape=jax.ShapeDtypeStruct((count, pieces, 8, 128), jnp.bfloat16),
+        in_specs=[pl.BlockSpec(memory_space=pl.ANY)],
+        out_specs=pl.BlockSpec(memory_space=pltpu.VMEM),
+        scratch_shapes=[
+            pltpu.VMEM((groups, count, shard, quarter), jnp.bfloat16),
+            pltpu.SemaphoreType.DMA,
+            pltpu.SemaphoreType.DMA((groups - 1,)),
+            pltpu.SemaphoreType.DMA((groups - 1,)),
+        ],
+        compiler_params=pltpu.CompilerParams(collective_id=0, has_side_effects=True),
+        cost_estimate=pl.CostEstimate(
+            flops=20000000000, bytes_accessed=50000000, transcendentals=0
+        ),
+        name="sum_quarters",
+    )(grads)
 
 
 def pick_kernel(index_ref, data_ref, out_ref):
@@ -152,18 +260,17 @@
         axis=2,
     )
     moments = jnp.transpose(moments, (1, 0, 2, 3, 4)).reshape(owners, 2 * capacity, 8, 128)
-    first_trip = jnp.concatenate([moments, to_chunks(basis.astype(jnp.bfloat16))], axis=1)
-    first_trip = exchange(first_trip)
+    sent = jnp.concatenate([moments, to_chunks(basis.astype(jnp.bfloat16))], axis=1)
+    sent, grads = lax.optimization_barrier((sent, grads))
+    first_trip = exchange(sent)
     moments = first_trip[:, : 2 * capacity].reshape(owners * capacity, 16, 128)
     old_basis = from_chunks(first_trip[:, 2 * capacity :], shard, rank_full)
     old_basis = old_basis.reshape(total_rows, rank_full)
     moments = pick(slots, moments).reshape(count, 2, 8, 128)
 
-    parts = jnp.transpose(grads[0].reshape(count, shard, groups, quarter), (2, 0, 1, 3))
-    parts = lax.all_to_all(parts, "dp", split_axis=0, concat_axis=0, tiled=True)
-    mine = jnp.sum(parts.astype(jnp.float32), axis=0).astype(jnp.bfloat16)
-
-    second_trip = exchange(jnp.concatenate([to_chunks(mine), moments], axis=1))
+    mine = sum_quarters(grads, groups)
+
+    second_trip = exchange(jnp.concatenate([mine, moments], axis=1))
     own = from_chunks(second_trip[:, :pieces], shard, quarter).reshape(total_rows, quarter)
     first_old = from_chunks(second_trip[:, pieces], rank_full, quarter).astype(jnp.float32)
     second_old = from_chunks(second_trip[:, pieces + 1], rank_full, quarter).astype(jnp.float32)
@@ -196,10 +303,6 @@
     )
     back_delta = from_chunks(third_trip[:, :pieces], shard, quarter)
     full_delta = lax.all_gather(back_delta, "dp", axis=2, tiled=True)
-    new_weight = (weight.astype(jnp.float32) - step_size * full_delta.astype(jnp.float32)).astype(
-        jnp.bfloat16
-    )
-
     spread = pick(source, third_trip[:, pieces]).reshape(owners, capacity, 8, 128)
     spread = jnp.transpose(exchange(spread), (1, 0, 2, 3))
     here_projected = from_chunks(spread, rank_full, quarter).astype(jnp.float32)
@@ -224,6 +327,9 @@
     )
     fresh = (solved * root).astype(jnp.bfloat16).reshape(owners, shard, rank_full)
     new_basis = exchange(fresh).astype(jnp.float32)
+    new_weight = (weight.astype(jnp.float32) - step_size * full_delta.astype(jnp.float32)).astype(
+        jnp.bfloat16
+    )
     return (new_weight, new_basis, first_out, second_out)
 
 

time: 263 us -> 201 us (0.76)
  waiting for transfers between devices: 93 us -> 45.8 us
  local copies, waits for them, and re-layouts: 11.6 us -> 4.79 us
  starting transfers between devices: 42.9 us -> 36.7 us
    pallas_call x0 -> x1, Pallas kernels: none -> 27.9 us  [sum_quarters(): pl.pallas_call(sum_kernel, out_shape=jax.ShapeDtypeStruct((count, pieces,...]
    all_to_all x4, waiting for transfers between devices: 72.9 us -> 45.7 us  [exchange(): lax.all_to_all(data, 'rows', split_axis=axis, concat_axis=axis, tiled=True)]
    pallas_call x1, Pallas kernels: 40.2 us -> 13.1 us  [inverse_factor(): pl.pallas_call(inverse_factor_kernel, out_shape=jax.ShapeDtypeStruct((siz...]
    all_to_all x1 -> x0, waiting for transfers between devices: 20 us -> none  [per_device(): parts = lax.all_to_all(parts, 'dp', split_axis=0, concat_axis=0, tiled=True)]
    all_to_all x1 -> x0, starting transfers between devices: 4.84 us -> none  [per_device(): parts = lax.all_to_all(parts, 'dp', split_axis=0, concat_axis=0, tiled=True)]
    another operation x1 -> x0, local copies, waits for them, and re-layouts: 3.39 us -> none  [per_device(): grads[0].reshape(count, shard, groups, quarter)]
  transfers between devices with their start and end apart: 7 -> 6, of which waited for: 4 -> 3; matrix products, arithmetic and copies ran while one was open for 9% -> 9% of each run, Pallas kernels for 16% -> 22%
where the time goes in v3:
time: 201 us
  Pallas kernels  45.8 us (23%)
  waiting for transfers between devices  45.8 us (23%)
  starting transfers between devices  36.7 us (18%)
  blocking collectives  28.9 us (14%)
  other arithmetic  15.8 us (8%)
  between operations  14.3 us (7%)
  matrix products  8.48 us (4%)
  local copies, waits for them, and re-layouts  4.79 us (2%)
    all_to_all x4, waiting for transfers between devices, exchange(): lax.all_to_all(data, 'rows', split_axis=axis, concat_axis=axis, tiled=True)  45.7 us
    all_to_all x4, starting transfers between devices, exchange(): lax.all_to_all(data, 'rows', split_axis=axis, concat_axis=axis, tiled=True)  36.6 us
    all_to_all x1, blocking collectives, exchange(): lax.all_to_all(data, 'rows', split_axis=axis, concat_axis=axis, tiled=True)  28.9 us
    pallas_call x1, Pallas kernels, sum_quarters(): pl.pallas_call(sum_kernel, out_shape=jax.ShapeDtypeStruct((count, pieces,...  27.9 us
    pallas_call x1, Pallas kernels, inverse_factor(): pl.pallas_call(inverse_factor_kernel, out_shape=jax.ShapeDtypeStruct((siz...  13.1 us
    pallas_call x2, Pallas kernels, pick(): pl.pallas_call(pick_kernel, out_shape=jax.ShapeDtypeStruct((index.shape[0...  4.78 us
    convert_element_type x1, other arithmetic, per_device(): (weight.astype(jnp.float32) - step_size * full_delta.astype(jnp.float32))...  4.72 us
  transfers between devices with their start and end apart: 6, of which 3 were waited for; matrix products, arithmetic and copies ran while one was open for 9% of the time, Pallas kernels for 22%

profile of v3, /device:TPU:1, one launch (start us, length us, event | category | flops | bytes accessed | tf_op | source)
XLA Modules:
  0.0 200.6 jit_solution(13747916788869430501)
XLA Ops:
  7.2 0.0 copy-start
  7.2 0.0 copy-start.4
  7.2 1.4 convert_element_type.71
  8.7 0.1 copy-done.4
  8.8 0.1 convert_element_type.69
  8.8 0.3 copy-done.2
  9.1 0.1 convert_element_type.70
  9.2 0.1 pad_maximum_fusion.1
  9.3 0.3 copy.25
  9.6 1.3 pad_maximum_fusion
  10.8 13.3 %all-to-all-start = ((bf16[64,12,8,128]{3,2,1,0:T(8,128)(2,1)}), bf16[64,12,8,128]{3,2,1,0:T(8,128)(2,1)S(1)}, u32[]{:S(2)}, u32[]{:S(2)}) async-start(bf16[64,12,8,128]{3,2,1,0:T(8,128)(2,1)} %pad_maximum_fusion), calls=%async_computation | async-start | bytes 3145728 | tf_op jit(solution)/shard_map/all_to_all | solution.py:236
  24.1 0.0 all-gather.5.cloned.1.call-start
  24.2 0.2 convert_reduce_fusion
  24.4 0.5 multiply_add_fusion.index_ref
  24.9 27.9 %sum_quarters.1 = bf16[64,4,8,128]{3,2,1,0:T(8,128)(2,1)} custom-call(bf16[1,64,16,1024]{3,2,1,0:T(8,128)(2,1)} %grads_ref), custom_call_target="tpu_custom_call" | custom-call | flops 20000000000 | bytes 50000000 | tf_op jit(solution)/shard_map/sum_quarters/pallas_call | solution.py:174
  52.8 11.1 %all-to-all-done = bf16[64,12,8,128]{3,2,1,0:T(8,128)(2,1)S(1)} async-done(((bf16[64,12,8,128]{3,2,1,0:T(8,128)(2,1)}), bf16[64,12,8,128]{3,2,1,0:T(8,128)(2,1)S(1)}, u32[]{:S(2)}, u32[]{:S(2)}) %all-to-all-start) | async-done | bytes 1572896 | tf_op jit(solution)/shard_map/all_to_all | solution.py:236
  63.9 1.1 slice.29
  65.0 2.2 %pick.2 = bf16[64,16,128]{2,1,0:T(8,128)(2,1)} custom-call(s32[64]{0:T(128)} %multiply_add_fusion.index_ref, bf16[256,16,128]{2,1,0:T(8,128)(2,1)} %bitcast.86), custom_call_target="tpu_custom_call" | custom-call | tf_op jit(solution)/shard_map/pick/pallas_call | solution.py:206
  67.2 1.0 pad_maximum_fusion.2
  68.3 28.9 %all_to_all.25 = bf16[64,6,8,128]{3,2,1,0:T(8,128)(2,1)S(1)} all-to-all(bf16[64,6,8,128]{3,2,1,0:T(8,128)(2,1)S(1)} %pad_maximum_fusion.2), channel_id=1, replica_groups=mesh['dp'=4,'rows'=64] {'rows'}, dimensions={0} | all-to-all | bytes 1572864 | tf_op jit(solution)/shard_map/all_to_all | solution.py:236
  97.2 0.8 slice.31
  98.0 0.0 all-gather.5.cloned.1.call-update
  98.0 0.6 dynamic_slice.4
  98.6 0.6 compare_select_fusion
  99.4 0.3 multiply_convert_fusion
  99.7 0.4 fusion.1
  100.2 0.9 pad_maximum_fusion.3
  101.1 6.2 %all-to-all-start.2 = ((bf16[64,5,8,128]{3,2,1,0:T(8,128)(2,1)}), bf16[64,5,8,128]{3,2,1,0:T(8,128)(2,1)S(1)}, u32[]{:S(2)}, u32[]{:S(2)}) async-start(bf16[64,5,8,128]{3,2,1,0:T(8,128)(2,1)} %pad_maximum_fusion.3), calls=%async_computation.2 | async-start | bytes 1310720 | tf_op jit(solution)/shard_map/all_to_all | solution.py:236
  107.3 0.7 select_reduce_fusion.index_ref
  107.9 19.5 %all-to-all-done.2 = bf16[64,5,8,128]{3,2,1,0:T(8,128)(2,1)S(1)} async-done(((bf16[64,5,8,128]{3,2,1,0:T(8,128)(2,1)}), bf16[64,5,8,128]{3,2,1,0:T(8,128)(2,1)S(1)}, u32[]{:S(2)}, u32[]{:S(2)}) %all-to-all-start.2) | async-done | bytes 655392 | tf_op jit(solution)/shard_map/all_to_all | solution.py:236
  127.4 0.7 slice_bitcast_fusion.data_ref
  128.1 2.6 %pick.3 = bf16[256,8,128]{2,1,0:T(8,128)(2,1)} custom-call(s32[256]{0:T(256)} %select_reduce_fusion.index_ref, bf16[64,8,128]{2,1,0:T(8,128)(2,1)} %slice_bitcast_fusion.data_ref), custom_call_target="tpu_custom_call" | custom-call | tf_op jit(solution)/shard_map/pick/pallas_call | solution.py:206
  130.7 6.3 %all-to-all-start.4 = ((bf16[64,4,8,128]{3,2,1,0:T(8,128)(2,1)}), bf16[64,4,8,128]{3,2,1,0:T(8,128)(2,1)S(1)}, u32[]{:S(2)}, u32[]{:S(2)}) async-start(bf16[64,4,8,128]{3,2,1,0:T(8,128)(2,1)} %bitcast.89), calls=%async_computation.4 | async-start | bytes 1048576 | tf_op jit(solution)/shard_map/all_to_all | solution.py:236
  137.0 0.0 all-gather.3.cloned.1.call-start
  137.0 0.8 slice.33
  137.8 0.0 all-gather.3.cloned.1.call-update
  137.9 0.0 all-gather.5.cloned.1.call-done
  137.9 2.3 %fusion.18 = f32[1024,256]{1,0:T(8,128)S(1)} fusion(bf16[1024,1024]{1,0:T(8,128)(2,1)} %all-gather.5.cloned.1.call-done, bf16[1024,256]{1,0:T(8,128)(2,1)S(1)} %copy-done), kind=kOutput, calls=%fused_computation.40 | convolution fusion | flops 536870912 | bytes 3670016 | tf_op jit(solution)/shard_map/dot_general | solution.py:320
  140.2 2.5 %fusion.19.gram_ref = f32[256,256]{1,0:T(8,128)} fusion(f32[1024,256]{1,0:T(8,128)S(1)} %fusion.18), kind=kOutput, calls=%fused_computation.41 | convolution fusion | flops 805306368 | bytes 1310720 | tf_op jit(solution)/shard_map/dot_general | solution.py:321
  142.8 13.1 %inverse_factor.1 = f32[256,256]{1,0:T(8,128)} custom-call(f32[256,256]{1,0:T(8,128)} %fusion.19.gram_ref), custom_call_target="tpu_custom_call" | custom-call | flops 20000000000 | bytes 524288 | tf_op jit(solution)/shard_map/inverse_factor/pallas_call | solution.py:106
  155.9 2.9 %fusion = bf16[1024,256]{1,0:T(8,128)(2,1)} fusion(f32[1024,256]{1,0:T(8,128)S(1)} %fusion.18, f32[256,256]{1,0:T(8,128)} %inverse_factor.1), kind=kOutput, calls=%fused_computation.5 | convolution fusion | flops 805830656 | bytes 1835008 | tf_op jit(solution)/shard_map/dot_general | solution.py:325
  158.8 10.8 %all-to-all-start.3 = ((bf16[64,16,256]{2,1,0:T(8,128)(2,1)}), bf16[64,16,256]{2,1,0:T(8,128)(2,1)}, u32[]{:S(2)}, u32[]{:S(2)}) async-start(bf16[64,16,256]{2,1,0:T(8,128)(2,1)} %bitcast.88), calls=%async_computation.3 | async-start | bytes 1048576 | tf_op jit(solution)/shard_map/all_to_all | solution.py:236
  169.6 0.2 compare_reduce_fusion
  169.8 0.1 convert_element_type.90
  170.0 1.7 fusion.3
  171.7 15.2 %all-to-all-done.3 = bf16[64,16,256]{2,1,0:T(8,128)(2,1)} async-done(((bf16[64,16,256]{2,1,0:T(8,128)(2,1)}), bf16[64,16,256]{2,1,0:T(8,128)(2,1)}, u32[]{:S(2)}, u32[]{:S(2)}) %all-to-all-start.3) | async-done | bytes 524320 | tf_op jit(solution)/shard_map/all_to_all | solution.py:236
  186.8 2.2 %convert_element_type.81 = f32[64,16,256]{2,1,0:T(8,128)} convert(bf16[64,16,256]{2,1,0:T(8,128)(2,1)} %all-to-all-done.3) | non-fusion elementwise | flops 262144 | bytes 1572864 | tf_op jit(solution)/shard_map/convert_element_type | solution.py:329
  189.0 4.7 %subtract_convert_fusion = bf16[64,16,1024]{2,1,0:T(8,128)(2,1)} fusion(bf16[64,16,1024]{2,1,0:T(8,128)(2,1)} %all-gather.3.cloned.1.call-done, bf16[64,16,1024]{2,1,0:T(8,128)(2,1)} %param.9), kind=kLoop, calls=%fused_computation | loop fusion | flops 5242880 | bytes 6291456 | tf_op jit(solution)/shard_map/convert_element_type | solution.py:330
  (21 shorter events, 0.1 us)
Async XLA Ops:
  7.2 130.7 %copy-start = (bf16[1024,256]{1,0:T(8,128)(2,1)S(1)}, bf16[1024,256]{1,0:T(8,128)(2,1)}, u32[]{:S(2)}) copy-start(bf16[1024,256]{1,0:T(8,128)(2,1)} %param.13) | copy-start | bytes 1572868
  7.2 1.6 copy-start.4
  7.2 1.9 copy-start.2
  10.8 13.3 %copy-start.8 = (s32[64]{0:T(128)S(1)}, s32[64]{0:T(128)}, u32[]{:S(2)}) copy-start(s32[64]{0:T(128)} %param.14) | copy-start | bytes 772
  10.8 53.1 %all-to-all-start = ((bf16[64,12,8,128]{3,2,1,0:T(8,128)(2,1)}), bf16[64,12,8,128]{3,2,1,0:T(8,128)(2,1)S(1)}, u32[]{:S(2)}, u32[]{:S(2)}) async-start(bf16[64,12,8,128]{3,2,1,0:T(8,128)(2,1)} %pad_maximum_fusion), calls=%async_computation | async-start | bytes 3145728 | tf_op jit(solution)/shard_map/all_to_all | solution.py:236
  24.1 113.8 %all-gather.5.cloned.1.call-start = ((), (), s32[]{:S(2)}) async-start(), calls=%async_computation.6 | async-start | bytes 2621440 | tf_op jit(solution)/shard_map/all_gather | solution.py:277
  52.8 14.4 %copy-start.6 = (bf16[64,4,8,128]{3,2,1,0:T(8,128)(2,1)S(1)}, bf16[64,4,8,128]{3,2,1,0:T(8,128)(2,1)}, u32[]{:S(2)}) copy-start(bf16[64,4,8,128]{3,2,1,0:T(8,128)(2,1)} %sum_quarters.1) | copy-start | bytes 1572868
  67.2 30.8 %copy-start.9 = (s32[64]{0:T(128)S(1)}, s32[64]{0:T(128)}, u32[]{:S(2)}) copy-start(s32[64]{0:T(128)} %param.15) | copy-start | bytes 772
  98.0 1.4 copy-start.1
  99.7 7.6 %copy-start.7 = (s32[64]{0:T(128)S(1)}, s32[64]{0:T(128)}, u32[]{:S(2)}) copy-start(s32[64]{0:T(128)} %multiply_add_fusion.index_ref) | copy-start | bytes 772
  101.1 26.3 %all-to-all-start.2 = ((bf16[64,5,8,128]{3,2,1,0:T(8,128)(2,1)}), bf16[64,5,8,128]{3,2,1,0:T(8,128)(2,1)S(1)}, u32[]{:S(2)}, u32[]{:S(2)}) async-start(bf16[64,5,8,128]{3,2,1,0:T(8,128)(2,1)} %pad_maximum_fusion.3), calls=%async_computation.2 | async-start | bytes 1310720 | tf_op jit(solution)/shard_map/all_to_all | solution.py:236
  130.7 28.1 %all-to-all-start.4 = ((bf16[64,4,8,128]{3,2,1,0:T(8,128)(2,1)}), bf16[64,4,8,128]{3,2,1,0:T(8,128)(2,1)S(1)}, u32[]{:S(2)}, u32[]{:S(2)}) async-start(bf16[64,4,8,128]{3,2,1,0:T(8,128)(2,1)} %bitcast.89), calls=%async_computation.4 | async-start | bytes 1048576 | tf_op jit(solution)/shard_map/all_to_all | solution.py:236
  137.0 52.0 %all-gather.3.cloned.1.call-start = ((), (), s32[]{:S(2)}) async-start(), calls=%async_computation.5 | async-start | bytes 2621440 | tf_op jit(solution)/shard_map/all_gather | solution.py:305
  155.9 14.0 %copy-start.3 = (f32[4,256,256]{2,1,0:T(8,128)S(1)}, f32[4,256,256]{2,1,0:T(8,128)}, u32[]{:S(2)}) copy-start(f32[4,256,256]{2,1,0:T(8,128)} %param.12) | copy-start | bytes 3145732
  158.8 11.2 %copy-start.5 = (f32[4,256,256]{2,1,0:T(8,128)S(1)}, f32[4,256,256]{2,1,0:T(8,128)}, u32[]{:S(2)}) copy-start(f32[4,256,256]{2,1,0:T(8,128)} %param.11) | copy-start | bytes 3145732
  158.8 28.1 %all-to-all-start.3 = ((bf16[64,16,256]{2,1,0:T(8,128)(2,1)}), bf16[64,16,256]{2,1,0:T(8,128)(2,1)}, u32[]{:S(2)}, u32[]{:S(2)}) async-start(bf16[64,16,256]{2,1,0:T(8,128)(2,1)} %bitcast.88), calls=%async_computation.3 | async-start | bytes 1048576 | tf_op jit(solution)/shard_map/all_to_all | solution.py:236
Sparse Core Ops, SparseCore 0:
  98.1 32.9 all-gather.4
  140.2 37.1 all-gather.2

commit v4 on v3

--- a/solution.py
+++ b/solution.py
@@ -1,3 +1,5 @@
+import functools
+
 import jax
 import jax.numpy as jnp
 from jax import lax
@@ -101,19 +103,150 @@
     lax.fori_loop(0, size // PANEL, panel, 0)
 
 
-def inverse_factor(gram):
-    size = gram.shape[0]
+def greet(groups):
+    me = lax.axis_index("dp")
+    barrier = pltpu.get_barrier_semaphore()
+    for d in range(1, groups):
+        pl.semaphore_signal(
+            barrier,
+            inc=1,
+            device_id={"dp": lax.rem(me + d, groups)},
+            device_id_type=pl.DeviceIdType.MESH,
+        )
+    pl.semaphore_wait(barrier, groups - 1)
+    return me
+
+
+def push(source, target, send_sem, recv_sem, peer):
+    copy = pltpu.make_async_remote_copy(
+        src_ref=source,
+        dst_ref=target,
+        send_sem=send_sem,
+        recv_sem=recv_sem,
+        device_id={"dp": peer},
+        device_id_type=pl.DeviceIdType.MESH,
+    )
+    copy.start()
+    return copy
+
+
+def refresh_kernel(
+    root, part_ref, out_ref, held_ref, whole_ref, grams_ref, gram_ref, inverse_ref, work_ref, sems
+):
+    total, rank_full = part_ref.shape
+    block = held_ref.shape[1]
+    groups = total // block
+    me = greet(groups)
+
+    def rows(ref, who):
+        return ref.at[pl.ds(pl.multiple_of(who * block, block), block)]
+
+    copies = []
+    for d in range(1, groups):
+        peer = lax.rem(me + d, groups)
+        copies.append(
+            push(rows(part_ref, peer), held_ref.at[d - 1], sems.at[0, d], sems.at[1, d], peer)
+        )
+    for copy in copies:
+        copy.wait()
+    mine = rows(part_ref, me)[...].astype(jnp.float32)
+    for d in range(1, groups):
+        mine = mine + held_ref[d - 1].astype(jnp.float32)
+    mine = mine.astype(jnp.bfloat16)
+    rows(whole_ref, me)[...] = mine
+    contract = (((0,), (0,)), ((), ()))
+    grams_ref[me] = lax.dot_general(mine, mine, contract, preferred_element_type=jnp.float32)
+    copies = []
+    for d in range(1, groups):
+        peer = lax.rem(me + d, groups)
+        copies.append(
+            push(rows(whole_ref, me), rows(whole_ref, me), sems.at[2, d], sems.at[3, d], peer)
+        )
+    for copy in copies:
+        copy.wait()
+    for d in range(1, groups):
+        who = lax.rem(me + d, groups)
+        other = rows(whole_ref, who)[...]
+        grams_ref[who] = lax.dot_general(
+            other, other, contract, preferred_element_type=jnp.float32
+        )
+    gram = grams_ref[0]
+    for b in range(1, groups):
+        gram = gram + grams_ref[b]
+    gram_ref[...] = gram
+    inverse_factor_kernel(gram_ref, inverse_ref, work_ref)
+    inverse = inverse_ref[...] * root
+    high = inverse.astype(jnp.bfloat16)
+    low = (inverse - high.astype(jnp.float32)).astype(jnp.bfloat16)
+    contract = (((1,), (1,)), ((), ()))
+    for b in range(groups):
+        data = whole_ref[b * block : (b + 1) * block]
+        fresh = lax.dot_general(data, high, contract, preferred_element_type=jnp.float32)
+        fresh += lax.dot_general(data, low, contract, preferred_element_type=jnp.float32)
+        fresh = fresh.reshape(block // 8, 8, rank_full)
+        for c in range(rank_full // 128):
+            piece = fresh[:, :, 128 * c : 128 * c + 128].astype(jnp.bfloat16)
+            out_ref[b * (block // 8) : (b + 1) * (block // 8), c] = piece
+
+
+def refresh(part, groups, root):
+    total, rank_full = part.shape
+    block = total // groups
     return pl.pallas_call(
-        inverse_factor_kernel,
-        out_shape=jax.ShapeDtypeStruct((size, size), jnp.float32),
+        functools.partial(refresh_kernel, root),
+        out_shape=jax.ShapeDtypeStruct((total // 8, rank_full // 128, 8, 128), jnp.bfloat16),
         in_specs=[pl.BlockSpec(memory_space=pltpu.VMEM)],
         out_specs=pl.BlockSpec(memory_space=pltpu.VMEM),
-        scratch_shapes=[pltpu.VMEM((size, 2 * size), jnp.float32)],
+        scratch_shapes=[
+            pltpu.VMEM((groups - 1, block, rank_full), jnp.bfloat16),
+            pltpu.VMEM((total, rank_full), jnp.bfloat16),
+            pltpu.VMEM((groups, rank_full, rank_full), jnp.float32),
+            pltpu.VMEM((rank_full, rank_full), jnp.float32),
+            pltpu.VMEM((rank_full, rank_full), jnp.float32),
+            pltpu.VMEM((rank_full, 2 * rank_full), jnp.float32),
+            pltpu.SemaphoreType.DMA((4, groups)),
+        ],
+        compiler_params=pltpu.CompilerParams(collective_id=1, has_side_effects=True),
         cost_estimate=pl.CostEstimate(
-            flops=20000000000, bytes_accessed=8 * size * size, transcendentals=0
+            flops=20000000000, bytes_accessed=50000000, transcendentals=0
         ),
-        name="inverse_factor",
-    )(gram)
+        name="refresh",
+    )(part)
+
+
+def gather_kernel(groups, mine_ref, out_ref, local_sem, send_sem, recv_sem):
+    quarter = mine_ref.shape[2]
+    me = greet(groups)
+    columns = out_ref.at[:, :, pl.ds(pl.multiple_of(me * quarter, quarter), quarter)]
+    copies = []
+    for d in range(1, groups):
+        peer = lax.rem(me + d, groups)
+        copies.append(push(mine_ref, columns, send_sem.at[d - 1], recv_sem.at[d - 1], peer))
+    own = pltpu.make_async_copy(mine_ref, columns, local_sem)
+    own.start()
+    own.wait()
+    for copy in copies:
+        copy.wait()
+
+
+def gather_quarters(mine, groups):
+    count, shard, quarter = mine.shape
+    return pl.pallas_call(
+        functools.partial(gather_kernel, groups),
+        out_shape=jax.ShapeDtypeStruct((count, shard, quarter * groups), mine.dtype),
+        in_specs=[pl.BlockSpec(memory_space=pltpu.VMEM)],
+        out_specs=pl.BlockSpec(memory_space=pl.ANY),
+        scratch_shapes=[
+            pltpu.SemaphoreType.DMA,
+            pltpu.SemaphoreType.DMA((groups - 1,)),
+            pltpu.SemaphoreType.DMA((groups - 1,)),
+        ],
+        compiler_params=pltpu.CompilerParams(collective_id=2, has_side_effects=True),
+        cost_estimate=pl.CostEstimate(
+            flops=20000000000, bytes_accessed=50000000, transcendentals=0
+        ),
+        name="gather_quarters",
+    )(mine)
 
 
 def sum_kernel(grads_ref, out_ref, held_ref, local_sem, send_sem, recv_sem):
@@ -274,7 +407,8 @@
     own = from_chunks(second_trip[:, :pieces], shard, quarter).reshape(total_rows, quarter)
     first_old = from_chunks(second_trip[:, pieces], rank_full, quarter).astype(jnp.float32)
     second_old = from_chunks(second_trip[:, pieces + 1], rank_full, quarter).astype(jnp.float32)
-    whole = lax.all_gather(own, "dp", axis=1, tiled=True)
+    sketch_part = lax.dynamic_slice_in_dim(sketch, lax.axis_index("dp") * quarter, quarter, 0)
+    part = jnp.dot(own, sketch_part, preferred_element_type=jnp.float32).astype(jnp.bfloat16)
 
     projected = (
         lax.dot_general(
@@ -292,19 +426,28 @@
         * inverse_root
     ).astype(jnp.bfloat16)
 
-    third_trip = exchange(
-        jnp.concatenate(
-            [
-                to_chunks(delta.reshape(owners, shard, quarter)),
-                to_chunks(projected.astype(jnp.bfloat16))[:, None],
-            ],
-            axis=1,
-        )
-    )
+    sent = jnp.concatenate(
+        [
+            to_chunks(delta.reshape(owners, shard, quarter)),
+            to_chunks(projected.astype(jnp.bfloat16))[:, None],
+        ],
+        axis=1,
+    )
+    sent, part = lax.optimization_barrier((sent, part))
+    third_trip = exchange(sent)
+    fresh = refresh(part, groups, root).reshape(owners, shard * rank_full // 1024, 8, 128)
+
+    spread = pick(source, third_trip[:, pieces]).reshape(owners, capacity, 8, 128)
+    sent = jnp.concatenate([spread, fresh], axis=1)
     back_delta = from_chunks(third_trip[:, :pieces], shard, quarter)
-    full_delta = lax.all_gather(back_delta, "dp", axis=2, tiled=True)
-    spread = pick(source, third_trip[:, pieces]).reshape(owners, capacity, 8, 128)
-    spread = jnp.transpose(exchange(spread), (1, 0, 2, 3))
+    sent, back_delta = lax.optimization_barrier((sent, back_delta))
+    fourth_trip = exchange(sent)
+    full_delta = gather_quarters(back_delta, groups)
+    new_weight = (weight.astype(jnp.float32) - step_size * full_delta.astype(jnp.float32)).astype(
+        jnp.bfloat16
+    )
+    new_basis = from_chunks(fourth_trip[:, capacity:], shard, rank_full).astype(jnp.float32)
+    spread = jnp.transpose(fourth_trip[:, :capacity], (1, 0, 2, 3))
     here_projected = from_chunks(spread, rank_full, quarter).astype(jnp.float32)
     matched = slots[:, None] == (here * capacity + jnp.arange(capacity, dtype=jnp.int32))[None, :]
     valid = jnp.any(matched, axis=0)[:, None, None]
@@ -317,19 +460,6 @@
         0.0,
     )
 
-    sample = jnp.dot(whole, sketch, preferred_element_type=jnp.float32)
-    gram = lax.dot_general(
-        sample, sample, (((0,), (0,)), ((), ())), precision=lax.Precision.HIGHEST
-    )
-    inverse = inverse_factor(gram)
-    solved = lax.dot_general(
-        sample, inverse, (((1,), (1,)), ((), ())), precision=lax.Precision.HIGHEST
-    )
-    fresh = (solved * root).astype(jnp.bfloat16).reshape(owners, shard, rank_full)
-    new_basis = exchange(fresh).astype(jnp.float32)
-    new_weight = (weight.astype(jnp.float32) - step_size * full_delta.astype(jnp.float32)).astype(
-        jnp.bfloat16
-    )
     return (new_weight, new_basis, first_out, second_out)
 
 

time: 201 us -> 190 us (0.945)
  Pallas kernels: 45.8 us -> 91.6 us
  blocking collectives: 28.9 us -> 0 us
  waiting for transfers between devices: 45.8 us -> 31.2 us
  between operations: 14.3 us -> 0.84 us
  matrix products: 8.48 us -> 2.92 us
  other arithmetic: 15.8 us -> 19.1 us
    pallas_call x1 -> x2, Pallas kernels: 13.1 us -> 58.9 us  [the longest x1 31.8 us: refresh(): pl.pallas_call(functools.partial(refresh_kernel, root), out_shape=jax.Sha...]
    all_to_all x1 -> x0, blocking collectives: 28.9 us -> none  [exchange(): lax.all_to_all(data, 'rows', split_axis=axis, concat_axis=axis, tiled=True)]
    all_to_all x4, waiting for transfers between devices: 45.7 us -> 31.2 us  [exchange(): lax.all_to_all(data, 'rows', split_axis=axis, concat_axis=axis, tiled=True)]
    dot_general x3 -> x1, matrix products: 7.71 us -> 1.1 us  [per_device(): jnp.dot(own, sketch_part, preferred_element_type=jnp.float32)]
    concatenate x0 -> x1, other arithmetic: none -> 2.27 us  [per_device(): sent = jnp.concatenate([spread, fresh], axis=1)]
  transfers between devices with their start and end apart: 6 -> 4, of which waited for: 3 -> 2; matrix products, arithmetic and copies ran while one was open for 9% -> 4% of each run, Pallas kernels for 22% -> 46%
where the time goes in v4:
time: 190 us
  Pallas kernels  91.6 us (48%)
  starting transfers between devices  38.1 us (20%)
  waiting for transfers between devices  31.2 us (16%)
  other arithmetic  19.1 us (10%)
  local copies, waits for them, and re-layouts  5.82 us (3%)
  matrix products  2.92 us (2%)
    all_to_all x4, starting transfers between devices, exchange(): lax.all_to_all(data, 'rows', split_axis=axis, concat_axis=axis, tiled=True)  38.1 us
    pallas_call x1, Pallas kernels, refresh(): pl.pallas_call(functools.partial(refresh_kernel, root), out_shape=jax.Sha...  31.8 us
    all_to_all x4, waiting for transfers between devices, exchange(): lax.all_to_all(data, 'rows', split_axis=axis, concat_axis=axis, tiled=True)  31.2 us
    pallas_call x1, Pallas kernels, sum_quarters(): pl.pallas_call(sum_kernel, out_shape=jax.ShapeDtypeStruct((count, pieces,...  27.9 us
    pallas_call x1, Pallas kernels, gather_quarters(): pl.pallas_call(functools.partial(gather_kernel, groups), out_shape=jax.Sh...  27.1 us
    pallas_call x2, Pallas kernels, pick(): pl.pallas_call(pick_kernel, out_shape=jax.ShapeDtypeStruct((index.shape[0...  4.81 us
    convert_element_type x1, other arithmetic, per_device(): (weight.astype(jnp.float32) - step_size * full_delta.astype(jnp.float32))...  4.72 us
  transfers between devices with their start and end apart: 4, of which 2 were waited for; matrix products, arithmetic and copies ran while one was open for 4% of the time, Pallas kernels for 46%

profile of v4, /device:TPU:1, one launch (start us, length us, event | category | flops | bytes accessed | tf_op | source)
XLA Modules:
  0.0 189.6 jit_solution(6944109952823685518)
XLA Ops:
  0.6 0.0 copy-start
  0.6 0.0 copy-start.2
  0.7 0.0 copy-start.1
  0.7 1.4 convert_element_type.81
  2.1 0.1 copy-done.2
  2.2 0.1 convert_element_type.79
  2.3 0.3 copy-done.1
  2.6 0.1 convert_element_type.80
  2.6 0.1 pad_maximum_fusion.1
  2.7 0.3 copy.25
  3.0 1.3 pad_maximum_fusion
  4.3 13.3 %all-to-all-start = ((bf16[64,12,8,128]{3,2,1,0:T(8,128)(2,1)}), bf16[64,12,8,128]{3,2,1,0:T(8,128)(2,1)S(1)}, u32[]{:S(2)}, u32[]{:S(2)}) async-start(bf16[64,12,8,128]{3,2,1,0:T(8,128)(2,1)} %pad_maximum_fusion), calls=%async_computation | async-start | bytes 3145728 | tf_op jit(solution)/shard_map/all_to_all | solution.py:369
  17.6 0.0 copy-done.6
  17.6 0.2 convert_reduce_fusion
  17.8 0.5 multiply_add_fusion.index_ref
  18.3 27.9 %sum_quarters.1 = bf16[64,4,8,128]{3,2,1,0:T(8,128)(2,1)} custom-call(bf16[1,64,16,1024]{3,2,1,0:T(8,128)(2,1)} %grads_ref), custom_call_target="tpu_custom_call" | custom-call | flops 20000000000 | bytes 50000000 | tf_op jit(solution)/shard_map/sum_quarters/pallas_call | solution.py:307
  46.2 11.2 %all-to-all-done = bf16[64,12,8,128]{3,2,1,0:T(8,128)(2,1)S(1)} async-done(((bf16[64,12,8,128]{3,2,1,0:T(8,128)(2,1)}), bf16[64,12,8,128]{3,2,1,0:T(8,128)(2,1)S(1)}, u32[]{:S(2)}, u32[]{:S(2)}) %all-to-all-start) | async-done | bytes 1572896 | tf_op jit(solution)/shard_map/all_to_all | solution.py:369
  57.4 1.1 slice.37
  58.5 2.2 %pick.2 = bf16[64,16,128]{2,1,0:T(8,128)(2,1)} custom-call(s32[64]{0:T(128)} %multiply_add_fusion.index_ref, bf16[256,16,128]{2,1,0:T(8,128)(2,1)} %bitcast.87), custom_call_target="tpu_custom_call" | custom-call | tf_op jit(solution)/shard_map/pick/pallas_call | solution.py:339
  60.7 2.1 %pad_maximum_fusion.3 = bf16[64,6,8,128]{3,2,1,0:T(8,128)(2,1)} fusion(bf16[64,2,8,128]{3,2,1,0:T(8,128)(2,1)} %bitcast.96, bf16[64,4,8,128]{3,2,1,0:T(8,128)(2,1)} %sum_quarters.1), kind=kLoop, calls=%fused_computation.14 | loop fusion | flops 393216 | bytes 1572864 | tf_op jit(solution)/shard_map/concatenate | solution.py:406
  62.8 6.3 %all-to-all-start.1 = ((bf16[64,6,8,128]{3,2,1,0:T(8,128)(2,1)}), bf16[64,6,8,128]{3,2,1,0:T(8,128)(2,1)}, u32[]{:S(2)}, u32[]{:S(2)}) async-start(bf16[64,6,8,128]{3,2,1,0:T(8,128)(2,1)} %pad_maximum_fusion.3), calls=%async_computation.1 | async-start | bytes 1572864 | tf_op jit(solution)/shard_map/all_to_all | solution.py:369
  69.1 0.6 dynamic_slice.7
  69.7 0.6 compare_select_fusion
  70.4 0.2 compare_reduce_fusion
  70.5 0.7 select_reduce_fusion.index_ref
  71.2 0.8 slice.36
  72.0 20.0 %all-to-all-done.1 = bf16[64,6,8,128]{3,2,1,0:T(8,128)(2,1)} async-done(((bf16[64,6,8,128]{3,2,1,0:T(8,128)(2,1)}), bf16[64,6,8,128]{3,2,1,0:T(8,128)(2,1)}, u32[]{:S(2)}, u32[]{:S(2)}) %all-to-all-start.1) | async-done | bytes 786464 | tf_op jit(solution)/shard_map/all_to_all | solution.py:369
  92.0 1.1 slice.39
  93.1 1.4 multiply_convert_fusion
  94.5 1.1 convolution_convert_fusion.part_ref
  95.6 1.0 convert_multiply_fusion.1
  96.6 0.4 fusion
  97.1 0.9 pad_maximum_fusion.4
  98.0 6.2 %all-to-all-start.2 = ((bf16[64,5,8,128]{3,2,1,0:T(8,128)(2,1)}), bf16[64,5,8,128]{3,2,1,0:T(8,128)(2,1)S(1)}, u32[]{:S(2)}, u32[]{:S(2)}) async-start(bf16[64,5,8,128]{3,2,1,0:T(8,128)(2,1)} %pad_maximum_fusion.4), calls=%async_computation.2 | async-start | bytes 1310720 | tf_op jit(solution)/shard_map/all_to_all | solution.py:369
  104.1 31.8 %refresh.1 = bf16[128,2,8,128]{3,2,1,0:T(8,128)(2,1)} custom-call(bf16[1024,256]{1,0:T(8,128)(2,1)} %convolution_convert_fusion.part_ref), custom_call_target="tpu_custom_call" | custom-call | flops 20000000000 | bytes 50000000 | tf_op jit(solution)/shard_map/refresh/pallas_call | solution.py:195
  135.9 0.0 all-to-all-done.2
  135.9 0.7 slice_bitcast_fusion.data_ref
  136.6 2.6 %pick.3 = bf16[256,8,128]{2,1,0:T(8,128)(2,1)} custom-call(s32[256]{0:T(256)} %select_reduce_fusion.index_ref, bf16[64,8,128]{2,1,0:T(8,128)(2,1)} %slice_bitcast_fusion.data_ref), custom_call_target="tpu_custom_call" | custom-call | tf_op jit(solution)/shard_map/pick/pallas_call | solution.py:339
  139.2 2.3 %pad_maximum_fusion.2 = bf16[64,8,8,128]{3,2,1,0:T(8,128)(2,1)} fusion(bf16[64,4,8,128]{3,2,1,0:T(8,128)(2,1)} %bitcast.99, bf16[64,4,8,128]{3,2,1,0:T(8,128)(2,1)} %bitcast.91), kind=kLoop, calls=%fused_computation.9 | loop fusion | flops 524288 | bytes 2097152 | tf_op jit(solution)/shard_map/concatenate | solution.py:441
  141.5 0.8 slice.42
  142.3 12.4 %all-to-all-start.3 = ((bf16[64,8,8,128]{3,2,1,0:T(8,128)(2,1)}), bf16[64,8,8,128]{3,2,1,0:T(8,128)(2,1)S(1)}, u32[]{:S(2)}, u32[]{:S(2)}) async-start(bf16[64,8,8,128]{3,2,1,0:T(8,128)(2,1)} %pad_maximum_fusion.2), calls=%async_computation.3 | async-start | bytes 2097152 | tf_op jit(solution)/shard_map/all_to_all | solution.py:369
  154.7 27.1 %gather_quarters.1 = bf16[64,16,1024]{2,1,0:T(8,128)(2,1)} custom-call(bf16[64,16,256]{2,1,0:T(8,128)(2,1)} %bitcast.98), custom_call_target="tpu_custom_call" | custom-call | flops 20000000000 | bytes 50000000 | tf_op jit(solution)/shard_map/gather_quarters/pallas_call | solution.py:234
  181.9 4.7 %subtract_convert_fusion = bf16[64,16,1024]{2,1,0:T(8,128)(2,1)} fusion(bf16[64,16,1024]{2,1,0:T(8,128)(2,1)} %gather_quarters.1, bf16[64,16,1024]{2,1,0:T(8,128)(2,1)} %param.9), kind=kLoop, calls=%fused_computation | loop fusion | flops 5242880 | bytes 6291456 | tf_op jit(solution)/shard_map/convert_element_type | solution.py:446
  186.6 0.0 all-to-all-done.3
  186.6 0.2 slice_convert_fusion
  186.8 1.1 convert_bitcast_fusion
  187.9 0.0 copy-done.3
  187.9 1.7 fusion.2
  (10 shorter events, 0.0 us)
Async XLA Ops:
  0.6 93.8 %copy-start = (bf16[1024,256]{1,0:T(8,128)(2,1)S(1)}, bf16[1024,256]{1,0:T(8,128)(2,1)}, u32[]{:S(2)}) copy-start(bf16[1024,256]{1,0:T(8,128)(2,1)} %param.13) | copy-start | bytes 1572868
  0.6 1.6 copy-start.2
  0.7 1.9 %copy-start.1 = (f32[4,256,256]{2,1,0:T(8,128)S(1)}, f32[4,256,256]{2,1,0:T(8,128)}, u32[]{:S(2)}) copy-start(f32[4,256,256]{2,1,0:T(8,128)} %param.12) | copy-start | bytes 3145732
  4.3 13.3 %copy-start.6 = (s32[64]{0:T(128)S(1)}, s32[64]{0:T(128)}, u32[]{:S(2)}) copy-start(s32[64]{0:T(128)} %param.14) | copy-start | bytes 772
  4.3 53.1 %all-to-all-start = ((bf16[64,12,8,128]{3,2,1,0:T(8,128)(2,1)}), bf16[64,12,8,128]{3,2,1,0:T(8,128)(2,1)S(1)}, u32[]{:S(2)}, u32[]{:S(2)}) async-start(bf16[64,12,8,128]{3,2,1,0:T(8,128)(2,1)} %pad_maximum_fusion), calls=%async_computation | async-start | bytes 3145728 | tf_op jit(solution)/shard_map/all_to_all | solution.py:369
  58.5 10.6 %copy-start.7 = (s32[64]{0:T(128)S(1)}, s32[64]{0:T(128)}, u32[]{:S(2)}) copy-start(s32[64]{0:T(128)} %param.15) | copy-start | bytes 772
  58.5 11.8 %copy-start.5 = (s32[64]{0:T(128)S(1)}, s32[64]{0:T(128)}, u32[]{:S(2)}) copy-start(s32[64]{0:T(128)} %multiply_add_fusion.index_ref) | copy-start | bytes 772
  62.8 29.2 %all-to-all-start.1 = ((bf16[64,6,8,128]{3,2,1,0:T(8,128)(2,1)}), bf16[64,6,8,128]{3,2,1,0:T(8,128)(2,1)}, u32[]{:S(2)}, u32[]{:S(2)}) async-start(bf16[64,6,8,128]{3,2,1,0:T(8,128)(2,1)} %pad_maximum_fusion.3), calls=%async_computation.1 | async-start | bytes 1572864 | tf_op jit(solution)/shard_map/all_to_all | solution.py:369
  72.0 24.6 %copy-start.4 = (bf16[64,4,8,128]{3,2,1,0:T(8,128)(2,1)S(1)}, bf16[64,4,8,128]{3,2,1,0:T(8,128)(2,1)}, u32[]{:S(2)}) copy-start(bf16[64,4,8,128]{3,2,1,0:T(8,128)(2,1)} %slice.36) | copy-start | bytes 1572868
  98.0 38.0 %all-to-all-start.2 = ((bf16[64,5,8,128]{3,2,1,0:T(8,128)(2,1)}), bf16[64,5,8,128]{3,2,1,0:T(8,128)(2,1)S(1)}, u32[]{:S(2)}, u32[]{:S(2)}) async-start(bf16[64,5,8,128]{3,2,1,0:T(8,128)(2,1)} %pad_maximum_fusion.4), calls=%async_computation.2 | async-start | bytes 1310720 | tf_op jit(solution)/shard_map/all_to_all | solution.py:369
  142.3 44.3 %all-to-all-start.3 = ((bf16[64,8,8,128]{3,2,1,0:T(8,128)(2,1)}), bf16[64,8,8,128]{3,2,1,0:T(8,128)(2,1)S(1)}, u32[]{:S(2)}, u32[]{:S(2)}) async-start(bf16[64,8,8,128]{3,2,1,0:T(8,128)(2,1)} %pad_maximum_fusion.2), calls=%async_computation.3 | async-start | bytes 2097152 | tf_op jit(solution)/shard_map/all_to_all | solution.py:369
  186.6 1.3 copy-start.3

commit v5 on v4

--- a/solution.py
+++ b/solution.py
@@ -214,38 +214,72 @@
     )(part)
 
 
-def gather_kernel(groups, mine_ref, out_ref, local_sem, send_sem, recv_sem):
+def gather_kernel(groups, stacked, mine_ref, out_ref, local_sem, send_sem, recv_sem):
+    count = mine_ref.shape[0]
+    half = count // 2
     quarter = mine_ref.shape[2]
-    me = greet(groups)
-    columns = out_ref.at[:, :, pl.ds(pl.multiple_of(me * quarter, quarter), quarter)]
-    copies = []
-    for d in range(1, groups):
-        peer = lax.rem(me + d, groups)
-        copies.append(push(mine_ref, columns, send_sem.at[d - 1], recv_sem.at[d - 1], peer))
-    own = pltpu.make_async_copy(mine_ref, columns, local_sem)
+    me = lax.axis_index("dp")
+    right = lax.rem(me + 1, groups)
+    left = lax.rem(me + groups - 1, groups)
+    barrier = pltpu.get_barrier_semaphore()
+    for peer in (left, right):
+        pl.semaphore_signal(
+            barrier, inc=1, device_id={"dp": peer}, device_id_type=pl.DeviceIdType.MESH
+        )
+    pl.semaphore_wait(barrier, 2)
+
+    def place(who, first, size):
+        if stacked:
+            return out_ref.at[who, pl.ds(first, size)]
+        columns = pl.ds(pl.multiple_of(who * quarter, quarter), quarter)
+        return out_ref.at[pl.ds(first, size), :, columns]
+
+    def send(way, h):
+        return push(
+            mine_ref.at[pl.ds(h * half, half)],
+            place(me, h * half, half),
+            send_sem.at[way, h],
+            recv_sem.at[way, h],
+            (right, left)[way],
+        )
+
+    copies = [send(0, 0), send(1, 1), send(0, 1), send(1, 0)]
+    own = pltpu.make_async_copy(mine_ref, place(me, 0, count), local_sem)
     own.start()
+    copies[0].wait_recv()
+    block = place(left, 0, half)
+    onward = push(block, block, send_sem.at[0, 2], recv_sem.at[0, 2], right)
+    copies[1].wait_recv()
+    block = place(right, half, half)
+    backward = push(block, block, send_sem.at[1, 2], recv_sem.at[1, 2], left)
+    copies[2].wait_recv()
+    copies[3].wait_recv()
+    for copy in copies:
+        copy.wait_send()
+    onward.wait()
+    backward.wait()
     own.wait()
-    for copy in copies:
-        copy.wait()
-
-
-def gather_quarters(mine, groups):
+
+
+def gather_quarters(mine, groups, stacked, number):
+    assert groups == 4
     count, shard, quarter = mine.shape
+    shape = (groups,) + mine.shape if stacked else (count, shard, quarter * groups)
     return pl.pallas_call(
-        functools.partial(gather_kernel, groups),
-        out_shape=jax.ShapeDtypeStruct((count, shard, quarter * groups), mine.dtype),
+        functools.partial(gather_kernel, groups, stacked),
+        out_shape=jax.ShapeDtypeStruct(shape, mine.dtype),
         in_specs=[pl.BlockSpec(memory_space=pltpu.VMEM)],
         out_specs=pl.BlockSpec(memory_space=pl.ANY),
         scratch_shapes=[
             pltpu.SemaphoreType.DMA,
-            pltpu.SemaphoreType.DMA((groups - 1,)),
-            pltpu.SemaphoreType.DMA((groups - 1,)),
+            pltpu.SemaphoreType.DMA((2, 3)),
+            pltpu.SemaphoreType.DMA((2, 3)),
         ],
-        compiler_params=pltpu.CompilerParams(collective_id=2, has_side_effects=True),
+        compiler_params=pltpu.CompilerParams(collective_id=number, has_side_effects=True),
         cost_estimate=pl.CostEstimate(
             flops=20000000000, bytes_accessed=50000000, transcendentals=0
         ),
-        name="gather_quarters",
+        name="gather_tiles" if stacked else "gather_quarters",
     )(mine)
 
 
@@ -393,17 +427,23 @@
         axis=2,
     )
     moments = jnp.transpose(moments, (1, 0, 2, 3, 4)).reshape(owners, 2 * capacity, 8, 128)
-    sent = jnp.concatenate([moments, to_chunks(basis.astype(jnp.bfloat16))], axis=1)
+    tile = lax.dynamic_slice_in_dim(
+        to_chunks(basis.astype(jnp.bfloat16)), lax.axis_index("dp"), 1, 1
+    )
+    sent = jnp.concatenate([moments, tile], axis=1)
     sent, grads = lax.optimization_barrier((sent, grads))
     first_trip = exchange(sent)
     moments = first_trip[:, : 2 * capacity].reshape(owners * capacity, 16, 128)
-    old_basis = from_chunks(first_trip[:, 2 * capacity :], shard, rank_full)
-    old_basis = old_basis.reshape(total_rows, rank_full)
+    tile = first_trip[:, 2 * capacity]
     moments = pick(slots, moments).reshape(count, 2, 8, 128)
 
     mine = sum_quarters(grads, groups)
 
-    second_trip = exchange(jnp.concatenate([mine, moments], axis=1))
+    sent = jnp.concatenate([mine, moments], axis=1)
+    sent, tile = lax.optimization_barrier((sent, tile))
+    second_trip = exchange(sent)
+    old_basis = jnp.transpose(gather_quarters(tile, groups, True, 3), (1, 0, 2, 3))
+    old_basis = from_chunks(old_basis, shard, rank_full).reshape(total_rows, rank_full)
     own = from_chunks(second_trip[:, :pieces], shard, quarter).reshape(total_rows, quarter)
     first_old = from_chunks(second_trip[:, pieces], rank_full, quarter).astype(jnp.float32)
     second_old = from_chunks(second_trip[:, pieces + 1], rank_full, quarter).astype(jnp.float32)
@@ -442,7 +482,7 @@
     back_delta = from_chunks(third_trip[:, :pieces], shard, quarter)
     sent, back_delta = lax.optimization_barrier((sent, back_delta))
     fourth_trip = exchange(sent)
-    full_delta = gather_quarters(back_delta, groups)
+    full_delta = gather_quarters(back_delta, groups, False, 2)
     new_weight = (weight.astype(jnp.float32) - step_size * full_delta.astype(jnp.float32)).astype(
         jnp.bfloat16
     )

time: 190 us -> 179 us (0.942)
  waiting for transfers between devices: 31.2 us -> 16.9 us
  starting transfers between devices: 38.1 us -> 41.9 us
  Pallas kernels: 91.6 us -> 93.7 us
    all_to_all x4, waiting for transfers between devices: 31.2 us -> 16.9 us  [exchange(): lax.all_to_all(data, 'rows', split_axis=axis, concat_axis=axis, tiled=True)]
    all_to_all x4, starting transfers between devices: 38.1 us -> 41.9 us  [exchange(): lax.all_to_all(data, 'rows', split_axis=axis, concat_axis=axis, tiled=True)]
    pallas_call x1 -> x2, Pallas kernels: 27.1 us -> 29.9 us  [gather_quarters(): pl.pallas_call(functools.partial(gather_kernel, groups, stacked), out_sha...]
  transfers between devices with their start and end apart: 4 -> 4, of which waited for: 2 -> 3; matrix products, arithmetic and copies ran while one was open for 4% -> 5% of each run, Pallas kernels for 46% -> 50%
where the time goes in v5:
time: 179 us; the launch traced here: 178 us
  Pallas kernels  93.7 us (52%)
  starting transfers between devices  41.9 us (23%)
  other arithmetic  17.4 us (10%)
  waiting for transfers between devices  16.9 us (9%)
  local copies, waits for them, and re-layouts  5.59 us (3%)
  matrix products  1.88 us (1%)
    all_to_all x4, starting transfers between devices, exchange(): lax.all_to_all(data, 'rows', split_axis=axis, concat_axis=axis, tiled=True)  41.9 us
    pallas_call x1, Pallas kernels, refresh(): pl.pallas_call(functools.partial(refresh_kernel, root), out_shape=jax.Sha...  31.1 us
    pallas_call x2, Pallas kernels, gather_quarters(): pl.pallas_call(functools.partial(gather_kernel, groups, stacked), out_sha...  29.9 us
    pallas_call x1, Pallas kernels, sum_quarters(): pl.pallas_call(sum_kernel, out_shape=jax.ShapeDtypeStruct((count, pieces,...  27.9 us
    all_to_all x4, waiting for transfers between devices, exchange(): lax.all_to_all(data, 'rows', split_axis=axis, concat_axis=axis, tiled=True)  16.9 us
    pallas_call x2, Pallas kernels, pick(): pl.pallas_call(pick_kernel, out_shape=jax.ShapeDtypeStruct((index.shape[0...  4.78 us
    convert_element_type x1, other arithmetic, per_device(): (weight.astype(jnp.float32) - step_size * full_delta.astype(jnp.float32))...  4.72 us
  transfers between devices with their start and end apart: 4, of which 3 were waited for; matrix products, arithmetic and copies ran while one was open for 5% of the time, Pallas kernels for 50%

profile of v5, /device:TPU:1, one launch (start us, length us, event | category | flops | bytes accessed | tf_op | source)
XLA Modules:
  0.0 178.2 jit_solution(5316036532802568615)
XLA Ops:
  0.6 0.0 copy-start
  0.6 0.0 copy-start.2
  0.7 1.4 convert_element_type.81
  2.1 0.1 copy-done.2
  2.2 0.1 convert_bitcast_fusion.2
  2.3 0.1 copy.28
  2.5 0.1 copy-done.1
  2.6 0.1 convert_bitcast_fusion.1
  2.6 0.1 copy.29
  2.8 0.2 pad_maximum_fusion.1
  3.0 0.0 copy-start.6
  3.0 0.0 copy-start.7
  3.0 1.1 pad_maximum_fusion
  4.1 13.2 %all-to-all-start = ((bf16[64,9,8,128]{3,2,1,0:T(8,128)(2,1)}), bf16[64,9,8,128]{3,2,1,0:T(8,128)(2,1)S(1)}, u32[]{:S(2)}, u32[]{:S(2)}) async-start(bf16[64,9,8,128]{3,2,1,0:T(8,128)(2,1)} %pad_maximum_fusion), calls=%async_computation | async-start | bytes 2359296 | tf_op jit(solution)/shard_map/all_to_all | solution.py:403
  17.3 0.6 dynamic_slice.11
  17.9 0.6 compare_select_fusion
  18.6 0.2 convert_reduce_fusion
  18.8 0.2 compare_reduce_fusion
  19.0 0.7 select_reduce_fusion.index_ref
  19.6 27.9 %sum_quarters.1 = bf16[64,4,8,128]{3,2,1,0:T(8,128)(2,1)} custom-call(bf16[1,64,16,1024]{3,2,1,0:T(8,128)(2,1)} %grads_ref), custom_call_target="tpu_custom_call" | custom-call | flops 20000000000 | bytes 50000000 | tf_op jit(solution)/shard_map/sum_quarters/pallas_call | solution.py:341
  47.5 1.1 all-to-all-done
  48.7 1.1 slice.36
  49.8 2.2 %pick.2 = bf16[64,16,128]{2,1,0:T(8,128)(2,1)} custom-call(s32[64]{0:T(128)} %copy-done.5, bf16[256,16,128]{2,1,0:T(8,128)(2,1)} %bitcast.92), custom_call_target="tpu_custom_call" | custom-call | tf_op jit(solution)/shard_map/pick/pallas_call | solution.py:373
  51.9 0.0 copy-done.4
  52.0 1.9 %pad_maximum_fusion.3 = bf16[64,6,8,128]{3,2,1,0:T(8,128)(2,1)} fusion(bf16[64,2,8,128]{3,2,1,0:T(8,128)(2,1)} %bitcast.100, bf16[64,4,8,128]{3,2,1,0:T(8,128)(2,1)S(1)} %copy-done.4), kind=kLoop, calls=%fused_computation.14 | loop fusion | flops 393216 | bytes 1572864 | tf_op jit(solution)/shard_map/concatenate | solution.py:442
  53.9 0.7 slice_bitcast_fusion.1.mine_ref
  54.5 10.1 %all-to-all-start.1 = ((bf16[64,6,8,128]{3,2,1,0:T(8,128)(2,1)}), bf16[64,6,8,128]{3,2,1,0:T(8,128)(2,1)S(1)}, u32[]{:S(2)}, u32[]{:S(2)}) async-start(bf16[64,6,8,128]{3,2,1,0:T(8,128)(2,1)} %pad_maximum_fusion.3), calls=%async_computation.1 | async-start | bytes 1572864 | tf_op jit(solution)/shard_map/all_to_all | solution.py:403
  64.7 8.6 %gather_tiles.1 = bf16[4,64,8,128]{3,2,1,0:T(8,128)(2,1)} custom-call(bf16[64,8,128]{2,1,0:T(8,128)(2,1)} %slice_bitcast_fusion.1.mine_ref), custom_call_target="tpu_custom_call" | custom-call | flops 20000000000 | bytes 50000000 | tf_op jit(solution)/shard_map/gather_tiles/pallas_call | solution.py:268
  73.3 1.1 copy.31
  74.4 13.2 %all-to-all-done.1 = bf16[64,6,8,128]{3,2,1,0:T(8,128)(2,1)S(1)} async-done(((bf16[64,6,8,128]{3,2,1,0:T(8,128)(2,1)}), bf16[64,6,8,128]{3,2,1,0:T(8,128)(2,1)S(1)}, u32[]{:S(2)}, u32[]{:S(2)}) %all-to-all-start.1) | async-done | bytes 786464 | tf_op jit(solution)/shard_map/all_to_all | solution.py:403
  87.7 0.3 multiply_convert_fusion
  88.0 1.1 convolution_convert_fusion.part_ref
  89.2 0.4 fusion
  89.6 0.9 pad_maximum_fusion.4
  90.5 6.2 %all-to-all-start.2 = ((bf16[64,5,8,128]{3,2,1,0:T(8,128)(2,1)}), bf16[64,5,8,128]{3,2,1,0:T(8,128)(2,1)S(1)}, u32[]{:S(2)}, u32[]{:S(2)}) async-start(bf16[64,5,8,128]{3,2,1,0:T(8,128)(2,1)} %pad_maximum_fusion.4), calls=%async_computation.2 | async-start | bytes 1310720 | tf_op jit(solution)/shard_map/all_to_all | solution.py:403
  96.7 31.1 %refresh.1 = bf16[128,2,8,128]{3,2,1,0:T(8,128)(2,1)} custom-call(bf16[1024,256]{1,0:T(8,128)(2,1)} %convolution_convert_fusion.part_ref), custom_call_target="tpu_custom_call" | custom-call | flops 20000000000 | bytes 50000000 | tf_op jit(solution)/shard_map/refresh/pallas_call | solution.py:195
  127.8 0.0 all-to-all-done.2
  127.9 0.7 slice_bitcast_fusion.data_ref
  128.5 2.6 %pick.3 = bf16[256,8,128]{2,1,0:T(8,128)(2,1)} custom-call(s32[256]{0:T(256)} %select_reduce_fusion.index_ref, bf16[64,8,128]{2,1,0:T(8,128)(2,1)} %slice_bitcast_fusion.data_ref), custom_call_target="tpu_custom_call" | custom-call | tf_op jit(solution)/shard_map/pick/pallas_call | solution.py:373
  131.1 2.3 %pad_maximum_fusion.2 = bf16[64,8,8,128]{3,2,1,0:T(8,128)(2,1)} fusion(bf16[64,4,8,128]{3,2,1,0:T(8,128)(2,1)} %bitcast.105, bf16[64,4,8,128]{3,2,1,0:T(8,128)(2,1)} %bitcast.95), kind=kLoop, calls=%fused_computation.9 | loop fusion | flops 524288 | bytes 2097152 | tf_op jit(solution)/shard_map/concatenate | solution.py:481
  133.4 0.8 slice.42
  134.2 12.4 %all-to-all-start.3 = ((bf16[64,8,8,128]{3,2,1,0:T(8,128)(2,1)}), bf16[64,8,8,128]{3,2,1,0:T(8,128)(2,1)S(1)}, u32[]{:S(2)}, u32[]{:S(2)}) async-start(bf16[64,8,8,128]{3,2,1,0:T(8,128)(2,1)} %pad_maximum_fusion.2), calls=%async_computation.3 | async-start | bytes 2097152 | tf_op jit(solution)/shard_map/all_to_all | solution.py:403
  146.6 21.3 %gather_quarters.1 = bf16[64,16,1024]{2,1,0:T(8,128)(2,1)} custom-call(bf16[64,16,256]{2,1,0:T(8,128)(2,1)} %bitcast.103), custom_call_target="tpu_custom_call" | custom-call | flops 20000000000 | bytes 50000000 | tf_op jit(solution)/shard_map/gather_quarters/pallas_call | solution.py:268
  167.9 4.7 %subtract_convert_fusion = bf16[64,16,1024]{2,1,0:T(8,128)(2,1)} fusion(bf16[64,16,1024]{2,1,0:T(8,128)(2,1)} %gather_quarters.1, bf16[64,16,1024]{2,1,0:T(8,128)(2,1)} %param.9), kind=kLoop, calls=%fused_computation | loop fusion | flops 5242880 | bytes 6291456 | tf_op jit(solution)/shard_map/convert_element_type | solution.py:486
  172.6 2.6 %all-to-all-done.3 = bf16[64,8,8,128]{3,2,1,0:T(8,128)(2,1)S(1)} async-done(((bf16[64,8,8,128]{3,2,1,0:T(8,128)(2,1)}), bf16[64,8,8,128]{3,2,1,0:T(8,128)(2,1)S(1)}, u32[]{:S(2)}, u32[]{:S(2)}) %all-to-all-start.3) | async-done | bytes 1048608 | tf_op jit(solution)/shard_map/all_to_all | solution.py:403
  175.2 0.2 slice_convert_fusion
  175.4 1.1 convert_bitcast_fusion
  176.5 1.7 fusion.2
  (14 shorter events, 0.1 us)
Async XLA Ops:
  0.6 87.4 %copy-start = (bf16[1024,256]{1,0:T(8,128)(2,1)S(1)}, bf16[1024,256]{1,0:T(8,128)(2,1)}, u32[]{:S(2)}) copy-start(bf16[1024,256]{1,0:T(8,128)(2,1)} %param.13) | copy-start | bytes 1572868
  0.6 1.6 copy-start.2
  0.7 1.9 %copy-start.1 = (f32[4,256,256]{2,1,0:T(8,128)S(1)}, f32[4,256,256]{2,1,0:T(8,128)}, u32[]{:S(2)}) copy-start(f32[4,256,256]{2,1,0:T(8,128)} %param.12) | copy-start | bytes 3145732
  3.0 14.3 %copy-start.6 = (s32[64]{0:T(128)S(1)}, s32[64]{0:T(128)}, u32[]{:S(2)}) copy-start(s32[64]{0:T(128)} %param.15) | copy-start | bytes 772
  3.0 15.6 %copy-start.7 = (s32[64]{0:T(128)S(1)}, s32[64]{0:T(128)}, u32[]{:S(2)}) copy-start(s32[64]{0:T(128)} %param.14) | copy-start | bytes 772
  4.1 44.5 %all-to-all-start = ((bf16[64,9,8,128]{3,2,1,0:T(8,128)(2,1)}), bf16[64,9,8,128]{3,2,1,0:T(8,128)(2,1)S(1)}, u32[]{:S(2)}, u32[]{:S(2)}) async-start(bf16[64,9,8,128]{3,2,1,0:T(8,128)(2,1)} %pad_maximum_fusion), calls=%async_computation | async-start | bytes 2359296 | tf_op jit(solution)/shard_map/all_to_all | solution.py:403
  18.8 28.7 %copy-start.5 = (s32[64]{0:T(128)}, s32[64]{0:T(128)S(1)}, u32[]{:S(2)}) copy-start(s32[64]{0:T(128)S(1)} %multiply_add_fusion.index_ref) | copy-start | bytes 772
  47.5 4.4 %copy-start.4 = (bf16[64,4,8,128]{3,2,1,0:T(8,128)(2,1)S(1)}, bf16[64,4,8,128]{3,2,1,0:T(8,128)(2,1)}, u32[]{:S(2)}) copy-start(bf16[64,4,8,128]{3,2,1,0:T(8,128)(2,1)} %sum_quarters.1) | copy-start | bytes 1572868
  54.5 33.1 %all-to-all-start.1 = ((bf16[64,6,8,128]{3,2,1,0:T(8,128)(2,1)}), bf16[64,6,8,128]{3,2,1,0:T(8,128)(2,1)S(1)}, u32[]{:S(2)}, u32[]{:S(2)}) async-start(bf16[64,6,8,128]{3,2,1,0:T(8,128)(2,1)} %pad_maximum_fusion.3), calls=%async_computation.1 | async-start | bytes 1572864 | tf_op jit(solution)/shard_map/all_to_all | solution.py:403
  90.5 37.3 %all-to-all-start.2 = ((bf16[64,5,8,128]{3,2,1,0:T(8,128)(2,1)}), bf16[64,5,8,128]{3,2,1,0:T(8,128)(2,1)S(1)}, u32[]{:S(2)}, u32[]{:S(2)}) async-start(bf16[64,5,8,128]{3,2,1,0:T(8,128)(2,1)} %pad_maximum_fusion.4), calls=%async_computation.2 | async-start | bytes 1310720 | tf_op jit(solution)/shard_map/all_to_all | solution.py:403
  134.2 40.9 %all-to-all-start.3 = ((bf16[64,8,8,128]{3,2,1,0:T(8,128)(2,1)}), bf16[64,8,8,128]{3,2,1,0:T(8,128)(2,1)S(1)}, u32[]{:S(2)}, u32[]{:S(2)}) async-start(bf16[64,8,8,128]{3,2,1,0:T(8,128)(2,1)} %pad_maximum_fusion.2), calls=%async_computation.3 | async-start | bytes 2097152 | tf_op jit(solution)/shard_map/all_to_all | solution.py:403
  175.2 1.3 copy-start.3
